TPU v7x, 256 devices: a whole 4x4x8 slice. The times are simulated.
256 devices in a mesh: section: 2 (over z_hi), dp: 16 (over z_lo, y), tensor: 8 (over x, core).
Axes of the slice: x: 4, y: 4, z: 8 (z_hi: 2, z_lo: 4; z = z_hi * 4 + z_lo), core: 2. Of those that a mesh axis runs over, the one named last changes fastest.
Arguments:
- section_input: bfloat16 [2, 1024, 8192], P('section', 'tensor', 'dp'), may hold values from -40 to 40
- norm_gain_attn: bfloat16 [2, 8192], P('section', 'dp'), may hold values from 0.099609375 to 1.8984375
- w_query: bfloat16 [2, 8192, 4096], P('section', 'dp', 'tensor'), may hold values from -0.0625 to 0.0625
- key_value_weight: bfloat16 [2, 2, 8192, 512], P('section', None, 'dp'), may hold values from -0.0625 to 0.0625
- w_output: bfloat16 [2, 4096, 8192], P('section', 'tensor', 'dp'), may hold values from -0.09375 to 0.09375
- norm_gain_ffn: bfloat16 [2, 8192], P('section', 'dp'), may hold values from 0.099609375 to 1.8984375
- w_gate_up: bfloat16 [2, 2, 8192, 14336], P('section', None, 'dp', 'tensor'), may hold values from -0.0625 to 0.0625
- w_down: bfloat16 [2, 14336, 8192], P('section', 'tensor', 'dp'), may hold values from -0.046875 to 0.046875
Outputs:
- section_output: bfloat16 [2, 1024, 8192], P('section', 'tensor', 'dp')
All inputs are finite; a program needn't handle non-finite values.
Results may differ from a plain program's by a relative error of at most 0.019.
Values may be sent and summed in bfloat16 or wider, within the bound.
A program may use at most 64 MiB of HBM per device.

v0:
```python
import math

import jax
import jax.numpy as jnp
from jax import lax
from jax.sharding import PartitionSpec as P

HEAD_SIZE = 128
QUERY_HEADS = 32
KEY_VALUE_HEADS = 4


EPS = 1e-05
THETA = 500000.0


def from_behind(x, axis, by):
    count = lax.axis_size(axis)
    return lax.ppermute(x, axis, [(i, (i + by) % count) for i in range(count)])


def apply_rotary(value_states, token_positions):
    width = value_states.shape[-1]
    half = width // 2
    freqs = jnp.exp(-(2.0 * jnp.arange(half, dtype=jnp.float32) / width) * math.log(THETA))
    angles = token_positions.astype(jnp.float32)[:, None] * freqs[None, :]
    cosine = jnp.cos(angles)[:, None, :]
    sine = jnp.sin(angles)[:, None, :]
    first = value_states[..., :half]
    second = value_states[..., half:]
    return jnp.concatenate(
        [first * cosine - second * sine, second * cosine + first * sine], axis=-1
    )


def local(
    section_input,
    norm_gain_attn,
    w_query,
    key_value_weight,
    w_output,
    norm_gain_ffn,
    w_gate_up,
    w_down,
):
    tile = section_input[0]
    rows_dev = tile.shape[0]
    cols_dev = tile.shape[1]
    tensor_count = lax.axis_size("tensor")
    data_count = lax.axis_size("dp")
    seq_total = rows_dev * tensor_count
    query_rows = seq_total // data_count
    width_total = cols_dev * data_count
    head_dim = HEAD_SIZE
    heads_dev = w_query.shape[2] // head_dim
    group_heads = QUERY_HEADS // KEY_VALUE_HEADS
    kv_dev = max(1, heads_dev // group_heads)
    per_kv = heads_dev // kv_dev
    tensor_pos = lax.axis_index("tensor")
    data_pos = lax.axis_index("dp")
    kv_first = tensor_pos * heads_dev // group_heads
    key_cols = lax.dynamic_slice_in_dim(
        key_value_weight[0], kv_first * head_dim, kv_dev * head_dim, 2
    )
    w_columns = jnp.concatenate([w_query[0], key_cols[0], key_cols[1]], axis=1)
    gain_attn = norm_gain_attn[0].astype(jnp.float32)[None, :]
    gain_ffn = norm_gain_ffn[0].astype(jnp.float32)[None, :]
    query_cols = heads_dev * head_dim
    kv_cols = kv_dev * head_dim
    query_pos = data_pos * query_rows + jnp.arange(query_rows, dtype=jnp.int32)
    all_pos = jnp.arange(seq_total, dtype=jnp.int32)
    arrived = from_behind(tile, "section", 1)
    wide = arrived.astype(jnp.float32)
    squares = lax.psum(jnp.sum(wide * wide, axis=1), "dp")
    normed_input = (wide * lax.rsqrt(squares / width_total + EPS)[:, None] * gain_attn).astype(
        jnp.bfloat16
    )
    partial_qkv = jnp.dot(
        lax.all_gather(normed_input, "tensor", axis=0, tiled=True),
        w_columns,
        preferred_element_type=jnp.float32,
    )
    query_sum = lax.psum_scatter(
        partial_qkv[:, :query_cols].astype(jnp.bfloat16), "dp", scatter_dimension=0, tiled=True
    ).astype(jnp.float32)
    key_sum = lax.psum(partial_qkv[:, query_cols:].astype(jnp.bfloat16), "dp").astype(jnp.float32)
    keys = apply_rotary(key_sum[:, :kv_cols].reshape(seq_total, kv_dev, head_dim), all_pos).astype(
        jnp.bfloat16
    )
    value_states = key_sum[:, kv_cols:].reshape(seq_total, kv_dev, head_dim).astype(jnp.bfloat16)
    query_states = apply_rotary(
        query_sum.reshape(query_rows, heads_dev, head_dim), query_pos
    ).astype(jnp.bfloat16)
    grouped = query_states.reshape(query_rows, kv_dev, per_kv, head_dim)
    scores = jnp.einsum(
        "qkgd,skd->kgqs", grouped, keys, preferred_element_type=jnp.float32
    ) * head_dim ** (-0.5)
    visible = all_pos[None, :] <= query_pos[:, None]
    weights_exp = jnp.where(visible, jnp.exp(scores), 0.0)
    probs = (weights_exp / jnp.sum(weights_exp, axis=-1, keepdims=True)).astype(jnp.bfloat16)
    mixed = (
        jnp.einsum("kgqs,skd->qkgd", probs, value_states, preferred_element_type=jnp.float32)
        .astype(jnp.bfloat16)
        .reshape(query_rows, query_cols)
    )
    attn_partial = jnp.dot(
        lax.all_gather(mixed, "dp", axis=0, tiled=True),
        w_output[0],
        preferred_element_type=jnp.float32,
    )
    attn = lax.psum_scatter(
        attn_partial.astype(jnp.bfloat16), "tensor", scatter_dimension=0, tiled=True
    ).astype(jnp.float32)
    resid = (arrived.astype(jnp.float32) + attn).astype(jnp.bfloat16)
    resid_wide = resid.astype(jnp.float32)
    squares_ffn = lax.psum(jnp.sum(resid_wide * resid_wide, axis=1), "dp")
    normed_ffn = (
        resid_wide * lax.rsqrt(squares_ffn / width_total + EPS)[:, None] * gain_ffn
    ).astype(jnp.bfloat16)
    rows_ffn = lax.all_gather(normed_ffn, "tensor", axis=0, tiled=True)
    ff_dev = w_gate_up.shape[3]
    summed = lax.psum_scatter(
        jnp.einsum("rd,gdf->rgf", rows_ffn, w_gate_up[0], preferred_element_type=jnp.float32)
        .reshape(query_rows * lax.axis_size("dp"), 2 * ff_dev)
        .astype(jnp.bfloat16),
        "dp",
        scatter_dimension=0,
        tiled=True,
    ).astype(jnp.float32)
    hidden = (jax.nn.silu(summed[:, :ff_dev]) * summed[:, ff_dev:]).astype(jnp.bfloat16)
    ffn_partial = jnp.dot(
        lax.all_gather(hidden, "dp", axis=0, tiled=True),
        w_down[0],
        preferred_element_type=jnp.float32,
    )
    ffn = lax.psum_scatter(
        ffn_partial.astype(jnp.bfloat16), "tensor", scatter_dimension=0, tiled=True
    ).astype(jnp.float32)
    result = (resid_wide + ffn).astype(jnp.bfloat16)
    return result[None]


def solution(mesh):
    placed = (
        P("section", "tensor", "dp"),
        P("section", "dp"),
        P("section", "dp", "tensor"),
        P("section", None, "dp", None),
        P("section", "tensor", "dp"),
        P("section", "dp"),
        P("section", None, "dp", "tensor"),
        P("section", "tensor", "dp"),
    )
    return jax.shard_map(
        local, mesh=mesh, in_specs=placed, out_specs=P("section", "tensor", "dp"), check_vma=False
    )
```

profile of v0, /device:TPU:1, one launch (start us, length us, event | category | flops | bytes accessed | tf_op | source)
XLA Modules:
  0.0 764.7 jit_solution(4502816704359785971)
XLA Ops:
  6.5 7.7 %collective-permute-start = (bf16[128,512]{1,0:T(8,128)(2,1)}, bf16[128,512]{1,0:T(8,128)(2,1)S(1)}, u32[]{:S(2)}, u32[]{:S(2)}) collective-permute-start(bf16[128,512]{1,0:T(8,128)(2,1)} %bitcast.70), channel_id=1, source_target_pairs={{0,128},{128,0},{1,129},{129,1},{2,130},{130,2},{3,131},{131,3},{4... | collective-permute-start | bytes 393224 | tf_op jit(solution)/shard_map/ppermute | solution.py:19
  14.3 0.7 mul.231
  15.0 2.3 collective-permute-done
  17.2 0.1 fusion.25
  17.3 36.4 %psum.21 = f32[128]{0:T(128)S(1)} all-reduce(f32[128]{0:T(128)S(1)} %fusion.25), channel_id=1, replica_groups=mesh['section'=2,'dp'=16,'tensor'=8] {'dp'}, use_global_device_ids=true, to_apply=%region_1.2 | all-reduce | flops 128 | bytes 1024 | tf_op jit(solution)/shard_map/psum | solution.py:74
  53.8 0.8 fusion.27
  54.6 0.0 all-reduce.2.cloned.1.call-start
  54.6 1.7 dynamic-slice_bitcast_fusion.1
  56.3 31.2 %all-gather.5.cloned.1.call-done = bf16[1024,512]{1,0:T(8,128)(2,1)} async-done(((bf16[128,512]{1,0:T(8,128)(2,1)}), bf16[1024,512]{1,0:T(8,128)(2,1)}) %all-gather.5.cloned.1.call-update) | async-done | bytes 1048592 | tf_op jit(solution)/shard_map/all_gather | solution.py:79
  87.5 2.4 convolution_convert_fusion.1
  90.0 0.8 slice.54
  90.8 0.0 all-reduce.2.cloned.1.call-update
  90.8 0.0 reduce-scatter.5.cloned.1.call-start
  90.9 1.0 slice.59
  92.0 0.0 all-gather.7.cloned.1.call-start
  92.1 0.1 iota_compare_fusion
  92.2 0.2 multiply_cosine_fusion.1
  92.4 149.4 %all-reduce.2.cloned.1.call-done = bf16[1024,256]{1,0:T(8,128)(2,1)} async-done(((bf16[1024,256]{1,0:T(8,128)(2,1)}), bf16[1024,256]{1,0:T(8,128)(2,1)}) %all-reduce.2.cloned.1.call-update) | async-done | bytes 524304 | tf_op jit(solution)/shard_map/psum | solution.py:86
  241.8 1.1 fusion.33
  242.8 2.4 fusion.37
  245.3 83.1 %reduce-scatter.5.cloned.1.call-done = bf16[64,512]{1,0:T(8,128)(2,1)} async-done(((bf16[1024,512]{1,0:T(8,128)(2,1)}), bf16[64,512]{1,0:T(8,128)(2,1)}) %reduce-scatter.5.cloned.1.call-update) | async-done | bytes 65552 | tf_op jit(solution)/shard_map/reduce_scatter | solution.py:83
  328.3 0.9 reshape.220
  329.2 0.1 fusion.45
  329.4 0.6 fusion.46
  330.0 0.4 fusion.8
  330.4 0.1 copy.13
  330.4 0.6 copy.23
  331.1 0.0 reduce-scatter.7.cloned.1.call-start
  331.1 78.1 %all-gather.7.cloned.1.call-done = bf16[1024,512]{1,0:T(8,128)(2,1)} async-done(((bf16[64,512]{1,0:T(8,128)(2,1)}), bf16[1024,512]{1,0:T(8,128)(2,1)}) %all-gather.7.cloned.1.call-update) | async-done | bytes 1048592 | tf_op jit(solution)/shard_map/all_gather | solution.py:107
  409.2 3.0 convolution_convert_fusion.2
  412.2 0.0 all-gather.9.cloned.1.call-start
  412.3 41.4 %reduce-scatter.7.cloned.1.call-done = bf16[128,512]{1,0:T(8,128)(2,1)} async-done(((bf16[1024,512]{1,0:T(8,128)(2,1)}), bf16[128,512]{1,0:T(8,128)(2,1)}) %reduce-scatter.7.cloned.1.call-update) | async-done | bytes 131088 | tf_op jit(solution)/shard_map/reduce_scatter | solution.py:111
  453.7 1.0 fusion.29
  454.7 36.1 %psum.23 = f32[128]{0:T(128)S(1)} all-reduce(f32[128]{0:T(128)S(1)} %fusion.29), channel_id=1, replica_groups=mesh['section'=2,'dp'=16,'tensor'=8] {'dp'}, use_global_device_ids=true, to_apply=%region_7.8 | all-reduce | flops 128 | bytes 1024 | tf_op jit(solution)/shard_map/psum | solution.py:116
  490.8 1.7 fusion.31
  492.5 0.0 reduce-scatter.9.cloned.1.call-start
  492.5 6.0 copy.14
  498.5 23.7 %all-gather.9.cloned.1.call-done = bf16[1024,512]{1,0:T(8,128)(2,1)} async-done(((bf16[128,512]{1,0:T(8,128)(2,1)}), bf16[1024,512]{1,0:T(8,128)(2,1)}) %all-gather.9.cloned.1.call-update) | async-done | bytes 1048592 | tf_op jit(solution)/shard_map/all_gather | solution.py:120
  522.2 9.3 %convolution_convert_fusion = bf16[1024,3584]{1,0:T(8,128)(2,1)} fusion(bf16[1024,512]{1,0:T(8,128)(2,1)} %all-gather.9.cloned.1.call-done, bf16[3584,512]{1,0:T(8,128)(2,1)} %bitcast.64), kind=kOutput, calls=%fused_computation | convolution fusion | flops 3761766400 | bytes 12058624 | tf_op jit(solution)/shard_map/rd,gdf->rgf/dot_general | solution.py:123
  531.6 0.0 all-gather.11.cloned.1.call-start
  531.6 94.9 %reduce-scatter.9.cloned.1.call-done = bf16[64,3584]{1,0:T(8,128)(2,1)} async-done(((bf16[1024,3584]{1,0:T(8,128)(2,1)}), bf16[64,3584]{1,0:T(8,128)(2,1)}) %reduce-scatter.9.cloned.1.call-update) | async-done | bytes 458768 | tf_op jit(solution)/shard_map/reduce_scatter | solution.py:122
  626.5 1.1 convert_element_type.103
  627.6 0.8 fusion.24
  628.4 0.0 reduce-scatter.11.cloned.1.call-start
  628.5 82.4 %all-gather.11.cloned.1.call-done = bf16[1024,1792]{1,0:T(8,128)(2,1)} async-done(((bf16[64,1792]{1,0:T(8,128)(2,1)}), bf16[1024,1792]{1,0:T(8,128)(2,1)}) %all-gather.11.cloned.1.call-update) | async-done | bytes 3670032 | tf_op jit(solution)/shard_map/all_gather | solution.py:132
  710.8 5.1 fusion.2
  715.9 40.6 %reduce-scatter.11.cloned.1.call-done = bf16[128,512]{1,0:T(8,128)(2,1)} async-done(((bf16[1024,512]{1,0:T(8,128)(2,1)}), bf16[128,512]{1,0:T(8,128)(2,1)}) %reduce-scatter.11.cloned.1.call-update) | async-done | bytes 131088 | tf_op jit(solution)/shard_map/reduce_scatter | solution.py:136
  756.6 1.6 fusion.38
  (25 shorter events, 0.2 us)
Async XLA Ops:
  6.5 704.3 %copy-start = (bf16[1,1792,512]{2,1,0:T(8,128)(2,1)S(1)}, bf16[1,1792,512]{2,1,0:T(8,128)(2,1)}, u32[]{:S(2)}) copy-start(bf16[1,1792,512]{2,1,0:T(8,128)(2,1)} %param.15) | copy-start | bytes 5505028
  6.5 81.0 %all-gather.5.cloned.1.call-start = ((), (), s32[]{:S(2)}) async-start(), calls=%async_computation.4 | async-start | bytes 1179648 | tf_op jit(solution)/shard_map/all_gather | solution.py:79
  6.5 10.7 %collective-permute-start = (bf16[128,512]{1,0:T(8,128)(2,1)}, bf16[128,512]{1,0:T(8,128)(2,1)S(1)}, u32[]{:S(2)}, u32[]{:S(2)}) collective-permute-start(bf16[128,512]{1,0:T(8,128)(2,1)} %bitcast.70), channel_id=1, source_target_pairs={{0,128},{128,0},{1,129},{129,1},{2,130},{130,2},{3,131},{131,3},{4... | collective-permute-start | bytes 393224 | tf_op jit(solution)/shard_map/ppermute | solution.py:19
  54.6 187.2 %all-reduce.2.cloned.1.call-start = ((), (), s32[]{:S(2)}) async-start(), calls=%async_computation.5 | async-start | bytes 1048576 | tf_op jit(solution)/shard_map/psum | solution.py:86
  90.8 237.5 %reduce-scatter.5.cloned.1.call-start = ((), (), s32[]{:S(2)}) async-start(), calls=%async_computation.6 | async-start | bytes 1114112 | tf_op jit(solution)/shard_map/reduce_scatter | solution.py:83
  92.0 317.2 %all-gather.7.cloned.1.call-start = ((), (), s32[]{:S(2)}) async-start(), calls=%async_computation.7 | async-start | bytes 1114112 | tf_op jit(solution)/shard_map/all_gather | solution.py:107
  241.8 88.2 %copy-start.2 = (bf16[1024,256]{1,0:T(8,128)(2,1)S(1)}, bf16[1024,256]{1,0:T(8,128)(2,1)}, u32[]{:S(2)}) copy-start(bf16[1024,256]{1,0:T(8,128)(2,1)} %all-reduce.2.cloned.1.call-done) | copy-start | bytes 1572868
  330.3 82.0 %copy-start.3 = (bf16[1,512]{1,0:T(2,128)(2,1)S(1)}, bf16[1,512]{1,0:T(2,128)(2,1)}, u32[]{:S(2)}) copy-start(bf16[1,512]{1,0:T(2,128)(2,1)} %param.13) | copy-start | bytes 3076
  331.1 122.6 %reduce-scatter.7.cloned.1.call-start = ((), (), s32[]{:S(2)}) async-start(), calls=%async_computation.8 | async-start | bytes 1179648 | tf_op jit(solution)/shard_map/reduce_scatter | solution.py:111
  412.2 110.0 %all-gather.9.cloned.1.call-start = ((), (), s32[]{:S(2)}) async-start(), calls=%async_computation.9 | async-start | bytes 1179648 | tf_op jit(solution)/shard_map/all_gather | solution.py:120
  492.5 134.0 %reduce-scatter.9.cloned.1.call-start = ((), (), s32[]{:S(2)}) async-start(), calls=%async_computation.10 | async-start | bytes 7798784 | tf_op jit(solution)/shard_map/reduce_scatter | solution.py:122
  531.6 179.2 %all-gather.11.cloned.1.call-start = ((), (), s32[]{:S(2)}) async-start(), calls=%async_computation.11 | async-start | bytes 3899392 | tf_op jit(solution)/shard_map/all_gather | solution.py:132
  628.4 128.2 %copy-start.1 = (bf16[128,512]{1,0:T(8,128)(2,1)S(1)}, bf16[128,512]{1,0:T(8,128)(2,1)}, u32[]{:S(2)}) copy-start(bf16[128,512]{1,0:T(8,128)(2,1)} %reduce-scatter.7.cloned.1.call-done) | copy-start | bytes 393220
  628.4 128.1 %reduce-scatter.11.cloned.1.call-start = ((), (), s32[]{:S(2)}) async-start(), calls=%async_computation.12 | async-start | bytes 1179648 | tf_op jit(solution)/shard_map/reduce_scatter | solution.py:136
Sparse Core Ops, SparseCore 0:
  54.7 32.7 all-gather.4
  91.0 150.7 all-reduce.1
  244.3 84.0 reduce-scatter.4
  331.2 77.9 all-gather.6
  412.4 41.2 reduce-scatter.6
  492.6 29.5 all-gather.8
  531.7 94.7 reduce-scatter.8
  628.5 82.2 all-gather.10
  716.1 40.4 reduce-scatter.10
where the time goes:
time: 767 us; the launch traced here: 765 us
  waiting for transfers between devices  627 us (82%)
  blocking collectives  72.5 us (9%)
  matrix products  20.8 us (3%)
  between operations  13.4 us (2%)
  other arithmetic  11.6 us (2%)
  local copies, waits for them, and re-layouts  11.3 us (1%)
  starting transfers between devices  8.06 us (1%)
    psum x1, waiting for transfers between devices, local(): lax.psum(partial_qkv[:, query_cols:].astype(jnp.bfloat16), 'dp')  149 us
    reduce_scatter x1, waiting for transfers between devices, local(): lax.psum_scatter(jnp.einsum('rd,gdf->rgf', rows_ffn, w_gate_up[0], prefer...  94.9 us
    reduce_scatter x1, waiting for transfers between devices, local(): lax.psum_scatter(partial_qkv[:, :query_cols].astype(jnp.bfloat16), 'dp',...  83.1 us
    all_gather x1, waiting for transfers between devices, local(): lax.all_gather(hidden, 'dp', axis=0, tiled=True)  82.4 us
    all_gather x1, waiting for transfers between devices, local(): lax.all_gather(mixed, 'dp', axis=0, tiled=True)  78.1 us
    reduce_scatter x1, waiting for transfers between devices, local(): lax.psum_scatter(attn_partial.astype(jnp.bfloat16), 'tensor', scatter_dim...  41.4 us
    reduce_scatter x1, waiting for transfers between devices, local(): lax.psum_scatter(ffn_partial.astype(jnp.bfloat16), 'tensor', scatter_dime...  40.6 us
    psum x1, blocking collectives, local(): squares = lax.psum(jnp.sum(wide * wide, axis=1), 'dp')  36.4 us
  transfers between devices with their start and end apart: 10, of which 10 were waited for; matrix products, arithmetic and copies ran while one was open for 2% of the time, Pallas kernels for 0%

commit v1 on v0

v1 whole, which is shorter than its diff:
```python
import functools
import math

import jax
import jax.numpy as jnp
import numpy as np
from jax import lax
from jax.experimental import pallas as pl
from jax.experimental.pallas import tpu as pltpu
from jax.sharding import PartitionSpec as P

HEAD = 128
EPS = 1e-05
THETA = 500000.0
RING = 4
ROWS = 64
GROUP = RING * ROWS
WIDTH = 8192
CHUNK = 256

MESH_ID = pl.DeviceIdType.MESH
BF = jnp.bfloat16
F32 = jnp.float32


class Place:
    def __init__(self):
        self.section = lax.axis_index("section")
        dp = lax.axis_index("dp")
        tensor = lax.axis_index("tensor")
        self.dp = dp
        self.z, self.y = lax.div(dp, RING), lax.rem(dp, RING)
        self.x, self.core = lax.div(tensor, 2), lax.rem(tensor, 2)

    def yi(self, k):
        return lax.rem(self.y + k, RING)

    def zi(self, k):
        return lax.rem(self.z + k, RING)

    def xi(self, k):
        return lax.rem(self.x + k, RING)

    def ydev(self, k):
        return {"dp": self.z * RING + self.yi(k)}

    def zdev(self, k):
        return {"dp": self.zi(k) * RING + self.y}

    def xdev(self, k):
        return {"tensor": self.xi(k) * 2 + self.core}

    def sibling(self):
        return {"tensor": self.x * 2 + 1 - self.core}

    def across(self):
        return {"section": 1 - self.section}


def enter(devices):
    barrier = pltpu.get_barrier_semaphore()
    for device in devices:
        pl.semaphore_signal(barrier, inc=1, device_id=device, device_id_type=MESH_ID)
    pl.semaphore_wait(barrier, len(devices))


def send(src, dst, sems, index, device):
    return pltpu.make_async_remote_copy(
        src_ref=src,
        dst_ref=dst,
        send_sem=sems[0].at[index],
        recv_sem=sems[1].at[index],
        device_id=device,
        device_id_type=MESH_ID,
    )


def gather_x(at, tokens, sems):
    def block(xx):
        return tokens.at[pl.ds(2 * at.core, 2), pl.ds(xx * ROWS, ROWS)]

    def half(xx, h):
        return tokens.at[2 * at.core + h, pl.ds(xx * ROWS, ROWS)]

    right, left, far = at.xi(1), at.xi(3), at.xi(2)
    go_right = send(block(at.x), block(at.x), sems, 0, at.xdev(1))
    go_left = send(block(at.x), block(at.x), sems, 1, at.xdev(3))
    share = send(block(at.x), block(at.x), sems, 2, at.sibling())
    go_right.start()
    go_left.start()
    share.start()
    go_right.wait_recv()
    pass_right = send(half(left, 0), half(left, 0), sems, 3, at.xdev(1))
    share_left = send(block(left), block(left), sems, 4, at.sibling())
    pass_right.start()
    share_left.start()
    go_left.wait_recv()
    pass_left = send(half(right, 1), half(right, 1), sems, 5, at.xdev(3))
    share_right = send(block(right), block(right), sems, 6, at.sibling())
    pass_left.start()
    share_right.start()
    pass_right.wait_recv()
    pass_left.wait_recv()
    share_far = send(block(far), block(far), sems, 7, at.sibling())
    share_far.start()
    share.wait_recv()
    share_left.wait_recv()
    share_right.wait_recv()
    share_far.wait_recv()
    return [go_right, go_left, share, pass_right, share_left, pass_left, share_right, share_far]


def scatter_x(at, part, pair, total, first, second, sems):
    mine, other = 2 * at.core, 2 * (1 - at.core)
    right, left, far = at.xi(1), at.xi(3), at.xi(2)

    def rows(xx):
        return pl.ds(xx * ROWS, ROWS)

    shares = []
    for i, xx in enumerate((far, right, left, at.x)):
        shares.append(
            send(part.at[pl.ds(other, 2), rows(xx)], pair.at[:, rows(xx)], sems, i, at.sibling())
        )
        shares[-1].start()

    def summed(i, xx):
        shares[i].wait_recv()
        return part[pl.ds(mine, 2), rows(xx)].astype(F32) + pair[:, rows(xx)].astype(F32)

    total[:, rows(far)] = summed(0, far).astype(BF)
    one_right = send(total.at[0, rows(far)], first.at[0], sems, 4, at.xdev(1))
    one_left = send(total.at[1, rows(far)], first.at[1], sems, 5, at.xdev(3))
    one_right.start()
    one_left.start()
    to_right = summed(1, right)
    one_right.wait_recv()
    total[0, rows(right)] = (to_right[0] + first[0].astype(F32)).astype(BF)
    total[1, rows(right)] = to_right[1].astype(BF)
    two_right = send(total.at[:, rows(right)], second.at[0], sems, 6, at.xdev(1))
    two_right.start()
    to_left = summed(2, left)
    one_left.wait_recv()
    total[0, rows(left)] = to_left[0].astype(BF)
    total[1, rows(left)] = (to_left[1] + first[1].astype(F32)).astype(BF)
    two_left = send(total.at[:, rows(left)], second.at[1], sems, 7, at.xdev(3))
    two_left.start()
    own = summed(3, at.x)
    two_right.wait_recv()
    two_left.wait_recv()
    tile = own + second[0].astype(F32) + second[1].astype(F32)
    return tile, shares + [one_right, one_left, two_right, two_left]


class Reduce:
    def __init__(self, at, part, first, second, third, sems_one, sems_two, sems_three):
        self.at = at
        self.part, self.first, self.second, self.third = part, first, second, third
        self.sems_one, self.sems_two, self.sems_three = sems_one, sems_two, sems_three

    def ones(self, c):
        far = self.at.yi(2)
        low, high = pl.ds(0, GROUP // 2), pl.ds(GROUP // 2, GROUP // 2)
        return (
            send(self.part.at[c, far, low], self.first.at[c, 0], self.sems_one, (c, 0), self.at.ydev(1)),
            send(self.part.at[c, far, high], self.first.at[c, 1], self.sems_one, (c, 1), self.at.ydev(3)),
        )

    def twos(self, c):
        return (
            send(self.part.at[c, self.at.yi(1)], self.second.at[c, 0], self.sems_two, (c, 0), self.at.ydev(1)),
            send(self.part.at[c, self.at.yi(3)], self.second.at[c, 1], self.sems_two, (c, 1), self.at.ydev(3)),
        )

    def threes(self, c):
        return [
            send(
                self.part.at[c, self.at.y, pl.ds(self.at.zi(k) * ROWS, ROWS)],
                self.third.at[c, k - 1],
                self.sems_three,
                (c, k - 1),
                self.at.zdev(k),
            )
            for k in (2, 1, 3)
        ]

    def far(self, c, product):
        self.part[c, self.at.yi(2)] = product(c, self.at.yi(2)).astype(BF)
        for copy in self.ones(c):
            copy.start()

    def near(self, c, product):
        half = GROUP // 2
        one, two = self.ones(c), self.twos(c)
        right, left = self.at.yi(1), self.at.yi(3)
        value = product(c, right)
        one[0].wait_recv()
        self.part[c, right, 0:half] = (value[:half] + self.first[c, 0].astype(F32)).astype(BF)
        self.part[c, right, half:GROUP] = value[half:].astype(BF)
        two[0].start()
        value = product(c, left)
        one[1].wait_recv()
        self.part[c, left, 0:half] = value[:half].astype(BF)
        self.part[c, left, half:GROUP] = (value[half:] + self.first[c, 1].astype(F32)).astype(BF)
        two[1].start()

    def own(self, c, product):
        value = product(c, self.at.y)
        two = self.twos(c)
        two[0].wait_recv()
        two[1].wait_recv()
        self.part[c, self.at.y] = (
            value + self.second[c, 0].astype(F32) + self.second[c, 1].astype(F32)
        ).astype(BF)
        for copy in self.threes(c):
            copy.start()

    def result(self, c):
        for copy in self.threes(c):
            copy.wait_recv()
        total = self.part[c, self.at.y, pl.ds(self.at.z * ROWS, ROWS)].astype(F32)
        for k in range(3):
            total = total + self.third[c, k].astype(F32)
        return total

    def drain(self, c):
        for copy in (*self.ones(c), *self.twos(c), *self.threes(c)):
            copy.wait_send()


class Gather:
    def __init__(self, at, whole, sems_line, sems_ring, sems_pass):
        self.at, self.whole = at, whole
        self.sems_line, self.sems_ring, self.sems_pass = sems_line, sems_ring, sems_pass

    def mine(self, c):
        return self.whole.at[c, self.at.y, pl.ds(self.at.z * ROWS, ROWS)]

    def lines(self, c):
        return [
            send(self.mine(c), self.mine(c), self.sems_line, (c, k - 1), self.at.zdev(k))
            for k in (2, 1, 3)
        ]

    def rings(self, c):
        block = self.whole.at[c, self.at.y]
        return [
            send(block, block, self.sems_ring, (c, 0), self.at.ydev(1)),
            send(block, block, self.sems_ring, (c, 1), self.at.ydev(3)),
        ]

    def passes(self, c):
        low = self.whole.at[c, self.at.yi(3), pl.ds(0, GROUP // 2)]
        high = self.whole.at[c, self.at.yi(1), pl.ds(GROUP // 2, GROUP // 2)]
        return [
            send(low, low, self.sems_pass, (c, 0), self.at.ydev(1)),
            send(high, high, self.sems_pass, (c, 1), self.at.ydev(3)),
        ]

    def line(self, c):
        for copy in self.lines(c):
            copy.start()

    def ring(self, c):
        for copy in self.lines(c):
            copy.wait_recv()
        for copy in self.rings(c):
            copy.start()

    def hand_on(self, c):
        for ring, onward in zip(self.rings(c), self.passes(c)):
            ring.wait_recv()
            onward.start()

    def finish(self, c):
        for copy in self.passes(c):
            copy.wait_recv()

    def drain(self, c):
        for copy in (*self.lines(c), *self.rings(c), *self.passes(c)):
            copy.wait_send()


class Squares:
    def __init__(self, at, part, near, mid, far, sems_y, sems_z):
        self.at, self.part, self.near, self.mid, self.far = at, part, near, mid, far
        self.sems_y, self.sems_z = sems_y, sems_z

    def fill(self, yy, wide):
        squared = (wide * wide).astype(BF)
        self.part[yy] = lax.dot_general(
            jnp.ones((8, wide.shape[1]), BF),
            squared,
            (((1,), (1,)), ((), ())),
            preferred_element_type=F32,
        )

    def ys(self):
        return [
            send(self.part.at[self.at.yi(k)], self.near.at[k - 1], self.sems_y, k - 1, self.at.ydev(k))
            for k in (1, 2, 3)
        ]

    def zs(self):
        return [
            send(self.mid, self.far.at[k - 1], self.sems_z, k - 1, self.at.zdev(k)) for k in (1, 2, 3)
        ]

    def start(self):
        for copy in self.ys():
            copy.start()

    def middle(self):
        for copy in self.ys():
            copy.wait_recv()
        self.mid[...] = self.part[self.at.y] + self.near[0] + self.near[1] + self.near[2]
        for copy in self.zs():
            copy.start()

    def scale(self):
        for copy in self.zs():
            copy.wait_recv()
        total = self.mid[...] + self.far[0] + self.far[1] + self.far[2]
        line = lax.rsqrt(total / WIDTH + EPS)[0:1]
        row = lax.broadcasted_iota(jnp.int32, (ROWS, GROUP), 0)
        lane = lax.broadcasted_iota(jnp.int32, (ROWS, GROUP), 1)
        picked = jnp.where(lane == row + self.at.z * ROWS, jnp.broadcast_to(line, (ROWS, GROUP)), 0.0)
        return jnp.sum(picked, axis=1, keepdims=True)

    def drain(self):
        for copy in (*self.ys(), *self.zs()):
            copy.wait_send()


def scaled(tokens, gain, out, squares, yy):
    wide = tokens[yy].astype(F32)
    squares.fill(yy, wide)
    out[yy] = (wide * gain).astype(BF)


def attend(
    src, gain_ref, wq_hbm, wkv_hbm, wo_hbm, table, out,
    tokens, normed, wq, wkv, wo,
    q_part, q_one, q_two, q_three, k_part, k_one, k_two, k_three,
    ss_part, ss_near, ss_mid, ss_far,
    keys, mixed, scores, part, pair, total, first, second,
    local, swap_s, swap_r, gx_s, gx_r, sx_s, sx_r, y_s, y_r, z_s, z_r,
    q1_s, q1_r, q2_s, q2_r, q3_s, q3_r, k1_s, k1_r, k2_s, k2_r, k3_s, k3_r,
    kl_s, kl_r, kr_s, kr_r, kp_s, kp_r, kc_s, kc_r, ml_s, ml_r, mr_s, mr_r, mp_s, mp_r,
):
    at = Place()
    loads = [
        pltpu.make_async_copy(wq_hbm, wq, local.at[0]),
        pltpu.make_async_copy(wkv_hbm.at[at.core, :, pl.ds(at.x * HEAD, HEAD)], wkv, local.at[1]),
        pltpu.make_async_copy(wo_hbm, wo, local.at[2]),
    ]
    for load in loads:
        load.start()
    enter(
        [at.ydev(k) for k in (1, 2, 3)]
        + [at.zdev(k) for k in (1, 2, 3)]
        + [at.xdev(1), at.xdev(3), at.sibling(), at.across()]
    )
    own_tile = tokens.at[pl.ds(2 * at.core, 2), pl.ds(at.x * ROWS, ROWS)]
    swap = send(src, own_tile, (swap_s, swap_r), 0, at.across())
    swap.start()
    gain = gain_ref[...].astype(F32)
    half = HEAD // 2
    lane = lax.broadcasted_iota(jnp.int32, (1, HEAD), 1)
    base = (table[0, pl.ds(ROWS + at.dp, 1), :], table[1, pl.ds(ROWS + at.dp, 1), :])
    step = (table[0, 0:ROWS, :], table[1, 0:ROWS, :])
    cosine = base[0] * step[0] - base[1] * step[1]
    sine = (base[1] * step[0] + base[0] * step[1]) * jnp.where(lane < half, -1.0, 1.0)
    for load in loads:
        load.wait()
    swap.wait_recv()
    pending = [swap] + gather_x(at, tokens, (gx_s, gx_r))

    squares = Squares(at, ss_part, ss_near, ss_mid, ss_far, (y_s, y_r), (z_s, z_r))
    qs = Reduce(at, q_part, q_one, q_two, q_three, (q1_s, q1_r), (q2_s, q2_r), (q3_s, q3_r))
    ks = Reduce(at, k_part, k_one, k_two, k_three, (k1_s, k1_r), (k2_s, k2_r), (k3_s, k3_r))

    def product_q(c, yy):
        return jnp.dot(normed[yy], wq[...], preferred_element_type=F32)

    def product_k(c, yy):
        return jnp.dot(normed[yy], wkv[...], preferred_element_type=F32)

    scaled(tokens, gain, normed, squares, at.yi(2))
    ks.far(0, product_k)
    qs.far(0, product_q)
    scaled(tokens, gain, normed, squares, at.yi(1))
    scaled(tokens, gain, normed, squares, at.yi(3))
    squares.start()
    ks.near(0, product_k)
    scaled(tokens, gain, normed, squares, at.y)
    qs.near(0, product_q)
    squares.middle()
    ks.own(0, product_k)
    scale = squares.scale()

    def rotated(value, cos, sin):
        return value * cos + pltpu.roll(value, half, 1) * sin

    is_key = at.core == 0
    whole = Gather(at, keys, (kl_s, kl_r), (kr_s, kr_r), (kp_s, kp_r))
    core = at.core
    value = ks.result(0) * scale
    keys[core, at.y, pl.ds(at.z * ROWS, ROWS)] = rotated(
        value, jnp.where(is_key, cosine, 1.0), jnp.where(is_key, sine, 0.0)
    ).astype(BF)
    key_sems = ((kl_s, kl_r), (kr_s, kr_r), (kc_s, kc_r))
    mine = keys.at[core, at.y, pl.ds(at.z * ROWS, ROWS)]
    lines = [send(mine, mine, key_sems[0], k - 1, at.zdev(k)) for k in (2, 1, 3)]
    for copy in lines:
        copy.start()
    qs.own(0, product_q)
    for copy in lines:
        copy.wait_recv()
    block = keys.at[core, at.y]
    rings = [send(block, block, key_sems[1], k - 1, at.ydev(k)) for k in (2, 1, 3)]
    shares = [send(block, block, key_sems[2], 0, at.sibling())]
    for copy in rings + shares:
        copy.start()
    for k, ring in zip((2, 1, 3), rings):
        ring.wait_recv()
        came = keys.at[core, at.yi(RING - k)]
        shares.append(send(came, came, key_sems[2], k, at.sibling()))
        shares[-1].start()
    pending += lines + rings + shares

    queries = qs.result(0) * scale
    stacked = jnp.concatenate(
        [rotated(queries[:, h * HEAD : (h + 1) * HEAD], cosine, sine) for h in range(4)], axis=0
    ).astype(BF)
    for copy in shares:
        copy.wait_recv()
    row = lax.broadcasted_iota(jnp.int32, (RING * ROWS, GROUP), 0)
    col = lax.broadcasted_iota(jnp.int32, (RING * ROWS, GROUP), 1)
    query_at = lax.rem(row, ROWS) + at.dp * ROWS
    key_at = lax.div(col, ROWS) * GROUP + lax.rem(col, ROWS)
    weight = jnp.zeros((RING * ROWS, 1), F32)
    for yy in range(RING):
        raw = lax.dot_general(
            stacked, keys[0, yy], (((1,), (1,)), ((), ())), preferred_element_type=F32
        ) * HEAD ** (-0.5)
        kept = jnp.where(key_at + yy * ROWS <= query_at, jnp.exp(raw), 0.0)
        scores[yy] = kept
        weight = weight + jnp.sum(kept, axis=1, keepdims=True)
    mix = jnp.zeros((RING * ROWS, HEAD), F32)
    for yy in range(RING):
        mix = mix + jnp.dot(
            (scores[yy] / weight).astype(BF), keys[1, yy], preferred_element_type=F32
        )
    for h in range(4):
        mixed[0, at.y, pl.ds(at.z * ROWS, ROWS), h * HEAD : (h + 1) * HEAD] = mix[
            h * ROWS : (h + 1) * ROWS
        ].astype(BF)

    heads = Gather(at, mixed, (ml_s, ml_r), (mr_s, mr_r), (mp_s, mp_r))
    heads.line(0)
    heads.ring(0)
    heads.hand_on(0)

    def project(yy):
        part[yy] = jnp.dot(mixed[0, yy], wo[...], preferred_element_type=F32).astype(BF)

    project(at.y)
    project(at.yi(1))
    project(at.yi(3))
    heads.finish(0)
    project(at.yi(2))
    tile, more = scatter_x(at, part, pair, total, first, second, (sx_s, sx_r))
    out[...] = (
        tokens[pl.ds(2 * at.core, 2), pl.ds(at.x * ROWS, ROWS)].astype(F32) + tile
    ).astype(BF)
    for copy in pending + more:
        copy.wait_send()
    squares.drain()
    qs.drain(0)
    ks.drain(0)
    heads.drain(0)


def feed(
    src, gain_ref, wgu_hbm, wd_hbm, out,
    tokens, normed, wgu, wd, h_part, h_one, h_two, h_three,
    ss_part, ss_near, ss_mid, ss_far, hidden, acc, part, pair, total, first, second,
    local, load_s, gx_s, gx_r, sx_s, sx_r, y_s, y_r, z_s, z_r,
    h1_s, h1_r, h2_s, h2_r, h3_s, h3_r, hl_s, hl_r, hr_s, hr_r, hp_s, hp_r,
):
    at = Place()
    chunks = wgu.shape[0]
    own_tile = tokens.at[pl.ds(2 * at.core, 2), pl.ds(at.x * ROWS, ROWS)]
    tile_in = pltpu.make_async_copy(src, own_tile, local.at[0])
    tile_in.start()
    down_in = pltpu.make_async_copy(wd_hbm, wd, local.at[1])
    loads = [
        pltpu.make_async_copy(
            wgu_hbm.at[g, :, pl.ds(c * CHUNK, CHUNK)], wgu.at[c, g], load_s.at[c, g]
        )
        for c in range(chunks)
        for g in range(2)
    ]
    for load in loads:
        load.start()
    down_in.start()
    enter(
        [at.ydev(k) for k in (1, 2, 3)]
        + [at.zdev(k) for k in (1, 2, 3)]
        + [at.xdev(1), at.xdev(3), at.sibling()]
    )
    tile_in.wait()
    gain = gain_ref[...].astype(F32)
    pending = gather_x(at, tokens, (gx_s, gx_r))
    for load in loads:
        load.wait()
    down_in.wait()
    squares = Squares(at, ss_part, ss_near, ss_mid, ss_far, (y_s, y_r), (z_s, z_r))
    hs = Reduce(at, h_part, h_one, h_two, h_three, (h1_s, h1_r), (h2_s, h2_r), (h3_s, h3_r))
    hg = Gather(at, hidden, (hl_s, hl_r), (hr_s, hr_r), (hp_s, hp_r))

    def product(c, yy):
        return jnp.concatenate(
            [jnp.dot(normed[yy], wgu[c, g], preferred_element_type=F32) for g in range(2)], axis=1
        )

    def each(body):
        lax.fori_loop(0, chunks, lambda c, carry: (body(c), carry)[1], 0)

    scaled(tokens, gain, normed, squares, at.yi(2))
    each(lambda c: hs.far(c, product))
    scaled(tokens, gain, normed, squares, at.yi(1))
    scaled(tokens, gain, normed, squares, at.yi(3))
    squares.start()
    scaled(tokens, gain, normed, squares, at.y)
    each(lambda c: hs.near(c, product))
    squares.middle()
    scale = squares.scale()
    each(lambda c: hs.own(c, product))

    def activate(c):
        both = hs.result(c) * scale
        gate, up = both[:, :CHUNK], both[:, CHUNK:]
        hidden[c, at.y, pl.ds(at.z * ROWS, ROWS)] = (gate / (1.0 + jnp.exp(-gate)) * up).astype(BF)
        hg.line(c)

    each(activate)
    each(hg.ring)
    each(hg.hand_on)

    def project(yy):
        acc[...] = jnp.zeros_like(acc)

        def body(c):
            acc[...] += jnp.dot(hidden[c, yy], wd[c], preferred_element_type=F32)

        each(body)
        part[yy] = acc[...].astype(BF)

    project(at.y)
    project(at.yi(1))
    project(at.yi(3))
    each(hg.finish)
    project(at.yi(2))
    tile, more = scatter_x(at, part, pair, total, first, second, (sx_s, sx_r))
    out[...] = (
        tokens[pl.ds(2 * at.core, 2), pl.ds(at.x * ROWS, ROWS)].astype(F32) + tile
    ).astype(BF)
    for copy in pending + more:
        copy.wait_send()
    squares.drain()
    each(hs.drain)
    each(hg.drain)


def pairs(*shapes):
    return [pltpu.SemaphoreType.DMA(shape) for shape in shapes for _ in range(2)]


def reduce_scratch(chunks, columns):
    return [
        pltpu.VMEM((chunks, RING, GROUP, columns), BF),
        pltpu.VMEM((chunks, 2, GROUP // 2, columns), BF),
        pltpu.VMEM((chunks, 2, GROUP, columns), BF),
        pltpu.VMEM((chunks, 3, ROWS, columns), BF),
    ]


def square_scratch():
    return [
        pltpu.VMEM((RING, 8, GROUP), F32),
        pltpu.VMEM((3, 8, GROUP), F32),
        pltpu.VMEM((8, GROUP), F32),
        pltpu.VMEM((3, 8, GROUP), F32),
    ]


def scatter_scratch(columns):
    return [
        pltpu.VMEM((RING, GROUP, columns), BF),
        pltpu.VMEM((2, GROUP, columns), BF),
        pltpu.VMEM((2, GROUP, columns), BF),
        pltpu.VMEM((2, ROWS, columns), BF),
        pltpu.VMEM((2, 2, ROWS, columns), BF),
    ]


def rotary_table(count):
    freq = np.exp(-(2.0 * np.arange(HEAD // 2) / HEAD) * math.log(THETA))
    position = np.concatenate([np.arange(ROWS), np.arange(count) * ROWS]).astype(np.float64)
    angle = position[:, None] * np.concatenate([freq, freq])[None, :]
    return np.stack([np.cos(angle), np.sin(angle)]).astype(np.float32)


def local_layer(
    section_input, gain_attn, w_query, key_value_weight, w_output, gain_ffn, w_gate_up, w_down
):
    cols = section_input.shape[2]
    heads = w_query.shape[2]
    ff = w_gate_up.shape[3]
    chunks = ff // CHUNK
    anywhere = pl.BlockSpec(memory_space=pl.ANY)
    vmem = pl.BlockSpec(memory_space=pltpu.VMEM)
    tile = jax.ShapeDtypeStruct((2, ROWS, cols), BF)
    limit = 60 * 1024 * 1024
    resid = pl.pallas_call(
        attend,
        name="attention_half",
        out_shape=tile,
        in_specs=[anywhere, vmem, anywhere, anywhere, anywhere, vmem],
        out_specs=vmem,
        scratch_shapes=[
            pltpu.VMEM((RING, GROUP, cols), BF),
            pltpu.VMEM((RING, GROUP, cols), BF),
            pltpu.VMEM((cols, heads), BF),
            pltpu.VMEM((cols, HEAD), BF),
            pltpu.VMEM((heads, cols), BF),
            *reduce_scratch(1, heads),
            *reduce_scratch(1, HEAD),
            *square_scratch(),
            pltpu.VMEM((2, RING, GROUP, HEAD), BF),
            pltpu.VMEM((1, RING, GROUP, heads), BF),
            pltpu.VMEM((RING, RING * ROWS, GROUP), F32),
            *scatter_scratch(cols),
            pltpu.SemaphoreType.DMA((3,)),
            *pairs((1,), (8,), (8,), (3,), (3,)),
            *pairs((1, 2), (1, 2), (1, 3), (1, 2), (1, 2), (1, 3)),
            *pairs((3,), (3,), (1,), (4,), (1, 3), (1, 2), (1, 2)),
        ],
        compiler_params=pltpu.CompilerParams(
            collective_id=0, has_side_effects=True, vmem_limit_bytes=limit
        ),
    )(
        section_input.reshape(2, ROWS, cols),
        gain_attn,
        w_query[0],
        key_value_weight[0],
        w_output[0],
        jnp.asarray(rotary_table(RING * RING)),
    )
    result = pl.pallas_call(
        feed,
        name="feed_forward_half",
        out_shape=tile,
        in_specs=[anywhere, vmem, anywhere, anywhere],
        out_specs=vmem,
        scratch_shapes=[
            pltpu.VMEM((RING, GROUP, cols), BF),
            pltpu.VMEM((RING, GROUP, cols), BF),
            pltpu.VMEM((chunks, 2, cols, CHUNK), BF),
            pltpu.VMEM((chunks, CHUNK, cols), BF),
            *reduce_scratch(chunks, 2 * CHUNK),
            *square_scratch(),
            pltpu.VMEM((chunks, RING, GROUP, CHUNK), BF),
            pltpu.VMEM((GROUP, cols), F32),
            *scatter_scratch(cols),
            pltpu.SemaphoreType.DMA((2,)),
            pltpu.SemaphoreType.DMA((chunks, 2)),
            *pairs((8,), (8,), (3,), (3,)),
            *pairs((chunks, 2), (chunks, 2), (chunks, 3)),
            *pairs((chunks, 3), (chunks, 2), (chunks, 2)),
        ],
        compiler_params=pltpu.CompilerParams(
            collective_id=1, has_side_effects=True, vmem_limit_bytes=limit
        ),
    )(resid, gain_ffn, w_gate_up[0], w_down[0].reshape(chunks, CHUNK, cols))
    return result.reshape(1, 2 * ROWS, cols)


def solution(mesh):
    placed = (
        P("section", "tensor", "dp"),
        P("section", "dp"),
        P("section", "dp", "tensor"),
        P("section", None, "dp", None),
        P("section", "tensor", "dp"),
        P("section", "dp"),
        P("section", None, "dp", "tensor"),
        P("section", "tensor", "dp"),
    )
    return jax.shard_map(
        local_layer, mesh=mesh, in_specs=placed, out_specs=P("section", "tensor", "dp"), check_vma=False
    )
```

time: 767 us -> 220 us (0.29)
  waiting for transfers between devices: 627 us -> 0 us
  Pallas kernels: 0 us -> 218 us
  blocking collectives: 72.5 us -> 0 us
  matrix products: 20.8 us -> 0 us
  between operations: 13.4 us -> 0.02 us
  other arithmetic: 11.6 us -> 0 us
  local copies, waits for them, and re-layouts: 11.3 us -> 1.57 us
  starting transfers between devices: 8.06 us -> 0 us
    reduce_scatter x4 -> x0, waiting for transfers between devices: 260 us -> none  [the longest x1 94.9 us: local(): lax.psum_scatter(jnp.einsum('rd,gdf->rgf', rows_ffn, w_gate_up[0], prefer...]
    pallas_call x0 -> x2, Pallas kernels: none -> 218 us  [the longest x1 139 us: local_layer(): pl.pallas_call(feed, name='feed_forward_half', out_shape=tile, in_specs=[...]
    all_gather x4 -> x0, waiting for transfers between devices: 215 us -> none  [the longest x1 82.4 us: local(): lax.all_gather(hidden, 'dp', axis=0, tiled=True)]
    psum x1 -> x0, waiting for transfers between devices: 149 us -> none  [local(): lax.psum(partial_qkv[:, query_cols:].astype(jnp.bfloat16), 'dp')]
    psum x2 -> x0, blocking collectives: 72.5 us -> none  [the longest x1 36.4 us: local(): squares = lax.psum(jnp.sum(wide * wide, axis=1), 'dp')]
    dot_general x6 -> x0, matrix products: 20.8 us -> none  [the longest x1 9.31 us: local(): jnp.einsum('rd,gdf->rgf', rows_ffn, w_gate_up[0], preferred_element_type=...]
    ppermute x1 -> x0, starting transfers between devices: 7.73 us -> none  [from_behind(): return lax.ppermute(x, axis, [(i, (i + by) % count) for i in range(count)])]
  transfers between devices with their start and end apart: 10 -> 0, of which waited for: 10 -> 0; matrix products, arithmetic and copies ran while one was open for 2% -> 0% of each run, Pallas kernels for 0% -> 0%
where the time goes in v1:
time: 220 us
  Pallas kernels  218 us (99%)
    pallas_call x1, Pallas kernels, local_layer(): pl.pallas_call(feed, name='feed_forward_half', out_shape=tile, in_specs=[...  139 us
    pallas_call x1, Pallas kernels, local_layer(): pl.pallas_call(attend, name='attention_half', out_shape=tile, in_specs=[a...  79.4 us

profile of v1, /device:TPU:1, one launch (start us, length us, event | category | flops | bytes accessed | tf_op | source)
XLA Modules:
  0.0 219.8 jit_solution(4263042893834220127)
XLA Ops:
  0.0 79.4 %attention_half.1.src = bf16[2,64,512]{2,1,0:T(8,128)(2,1)} custom-call(bf16[2,64,512]{2,1,0:T(8,128)(2,1)} %bitcast.13, bf16[1,512]{1,0:T(2,128)(2,1)} %gain_ref.2, bf16[512,512]{1,0:T(8,128)(2,1)} %bitcast.10, bf16[2,512,512]{2,1,0:T(8,128)(2,1)} %bitcast.9, bf16[512,512]{1,0:T(8,128)(2,1)} %bitcast.11, f32[2,80,128]{2,1,0:T(8,128)} %constant.2.clone.table), custom_call_target="tpu_custom_call" | custom-call | tf_op jit(solution)/shard_map/attention_half/pallas_call | solution.py:627
  79.4 138.8 %feed_forward_half.1 = bf16[2,64,512]{2,1,0:T(8,128)(2,1)} custom-call(bf16[2,64,512]{2,1,0:T(8,128)(2,1)} %attention_half.1.src, bf16[1,512]{1,0:T(2,128)(2,1)} %gain_ref.3, bf16[2,512,1792]{2,1,0:T(8,128)(2,1)} %bitcast.7, bf16[7,256,512]{2,1,0:T(8,128)(2,1)} %bitcast.8), custom_call_target="tpu_custom_call" | custom-call | tf_op jit(solution)/shard_map/feed_forward_half/pallas_call | solution.py:662
  218.2 1.6 copy.11

commit v2 on v1

v2 whole, which is shorter than its diff:
```python
import functools
import math
import types

import jax
import jax.numpy as jnp
import numpy as np
from jax import lax
from jax.experimental import pallas as pl
from jax.experimental.pallas import tpu as pltpu
from jax.sharding import PartitionSpec as P

HEAD = 128
EPS = 1e-05
THETA = 500000.0
RING = 4
ROWS = 64
GROUP = RING * ROWS
WIDTH = 8192

MESH_ID = pl.DeviceIdType.MESH
BF = jnp.bfloat16
F32 = jnp.float32


class Place:
    def __init__(self):
        self.section = lax.axis_index("section")
        dp = lax.axis_index("dp")
        tensor = lax.axis_index("tensor")
        self.dp = dp
        self.z, self.y = lax.div(dp, RING), lax.rem(dp, RING)
        self.x, self.core = lax.div(tensor, 2), lax.rem(tensor, 2)

    def yi(self, k):
        return lax.rem(self.y + k, RING)

    def zi(self, k):
        return lax.rem(self.z + k, RING)

    def xi(self, k):
        return lax.rem(self.x + k, RING)

    def ydev(self, k):
        return {"dp": self.z * RING + self.yi(k)}

    def zdev(self, k):
        return {"dp": self.zi(k) * RING + self.y}

    def xdev(self, k):
        return {"tensor": self.xi(k) * 2 + self.core}

    def sibling(self):
        return {"tensor": self.x * 2 + 1 - self.core}

    def across(self):
        return {"section": 1 - self.section}


def enter(devices):
    barrier = pltpu.get_barrier_semaphore()
    for device in devices:
        pl.semaphore_signal(barrier, inc=1, device_id=device, device_id_type=MESH_ID)
    pl.semaphore_wait(barrier, len(devices))


def send(src, dst, sems, index, device):
    return pltpu.make_async_remote_copy(
        src_ref=src,
        dst_ref=dst,
        send_sem=sems[0].at[index],
        recv_sem=sems[1].at[index],
        device_id=device,
        device_id_type=MESH_ID,
    )


class Spread:
    def __init__(self, at, tokens, sems):
        self.at = at
        self.right, self.left, self.far = at.xi(1), at.xi(3), at.xi(2)

        def block(xx):
            return tokens.at[pl.ds(2 * at.core, 2), pl.ds(xx * ROWS, ROWS)]

        def half(xx, h):
            return tokens.at[2 * at.core + h, pl.ds(xx * ROWS, ROWS)]

        def same(ref, index, device):
            return send(ref, ref, sems, index, device)

        self.out = [
            same(block(at.x), 0, at.xdev(1)),
            same(block(at.x), 1, at.xdev(3)),
            same(block(at.x), 2, at.sibling()),
        ]
        self.after_left = [
            same(half(self.left, 0), 3, at.xdev(1)),
            same(block(self.left), 4, at.sibling()),
        ]
        self.after_right = [
            same(half(self.right, 1), 5, at.xdev(3)),
            same(block(self.right), 6, at.sibling()),
        ]
        self.last = [same(block(self.far), 7, at.sibling())]

    def start(self):
        for copy in self.out:
            copy.start()

    def onward(self):
        self.out[0].wait_recv()
        for copy in self.after_left:
            copy.start()
        self.out[1].wait_recv()
        for copy in self.after_right:
            copy.start()

    def end(self):
        self.after_left[0].wait_recv()
        self.after_right[0].wait_recv()
        self.last[0].start()

    def finish(self):
        for copy in (self.out[2], self.after_left[1], self.after_right[1], self.last[0]):
            copy.wait_recv()

    def copies(self):
        return [*self.out, *self.after_left, *self.after_right, *self.last]


def scatter_x(at, part, pair, total, first, second, sems):
    mine, other = 2 * at.core, 2 * (1 - at.core)
    right, left, far = at.xi(1), at.xi(3), at.xi(2)

    def rows(xx):
        return pl.ds(xx * ROWS, ROWS)

    shares = []
    for i, xx in enumerate((far, right, left, at.x)):
        shares.append(
            send(part.at[pl.ds(other, 2), rows(xx)], pair.at[:, rows(xx)], sems, i, at.sibling())
        )
        shares[-1].start()

    def summed(i, xx):
        shares[i].wait_recv()
        return part[pl.ds(mine, 2), rows(xx)].astype(F32) + pair[:, rows(xx)].astype(F32)

    total[:, rows(far)] = summed(0, far).astype(BF)
    one_right = send(total.at[0, rows(far)], first.at[0], sems, 4, at.xdev(1))
    one_left = send(total.at[1, rows(far)], first.at[1], sems, 5, at.xdev(3))
    one_right.start()
    one_left.start()
    to_right = summed(1, right)
    one_right.wait_recv()
    total[0, rows(right)] = (to_right[0] + first[0].astype(F32)).astype(BF)
    total[1, rows(right)] = to_right[1].astype(BF)
    two_right = send(total.at[:, rows(right)], second.at[0], sems, 6, at.xdev(1))
    two_right.start()
    to_left = summed(2, left)
    one_left.wait_recv()
    total[0, rows(left)] = to_left[0].astype(BF)
    total[1, rows(left)] = (to_left[1] + first[1].astype(F32)).astype(BF)
    two_left = send(total.at[:, rows(left)], second.at[1], sems, 7, at.xdev(3))
    two_left.start()
    own = summed(3, at.x)
    two_right.wait_recv()
    two_left.wait_recv()
    tile = own + second[0].astype(F32) + second[1].astype(F32)
    return tile, shares + [one_right, one_left, two_right, two_left]


class Reduce:
    def __init__(self, at, part, first, second, third, sems, hand):
        self.at = at
        self.part, self.first, self.second, self.third = part, first, second, third
        self.sems_one, self.sems_two, self.sems_three = sems
        self.hand = hand

    def ones(self, c):
        far = self.at.yi(2)
        low, high = pl.ds(0, GROUP // 2), pl.ds(GROUP // 2, GROUP // 2)
        return (
            send(self.part.at[c, far, low], self.first.at[c, 0], self.sems_one, (c, 0), self.at.ydev(1)),
            send(self.part.at[c, far, high], self.first.at[c, 1], self.sems_one, (c, 1), self.at.ydev(3)),
        )

    def twos(self, c):
        return (
            send(self.part.at[c, self.at.yi(1)], self.second.at[c, 0], self.sems_two, (c, 0), self.at.ydev(1)),
            send(self.part.at[c, self.at.yi(3)], self.second.at[c, 1], self.sems_two, (c, 1), self.at.ydev(3)),
        )

    def threes(self, c):
        return [
            send(
                self.part.at[c, self.at.y, rows], self.third.at[c, slot], self.sems_three, (c, slot), device
            )
            for slot, rows, device in self.hand
        ]

    def far(self, c, product):
        self.part[c, self.at.yi(2)] = product(c, self.at.yi(2)).astype(BF)
        for copy in self.ones(c):
            copy.start()

    def near(self, c, product):
        half = GROUP // 2
        one, two = self.ones(c), self.twos(c)
        right, left = self.at.yi(1), self.at.yi(3)
        value = product(c, right)
        one[0].wait_recv()
        self.part[c, right, 0:half] = (value[:half] + self.first[c, 0].astype(F32)).astype(BF)
        self.part[c, right, half:GROUP] = value[half:].astype(BF)
        two[0].start()
        value = product(c, left)
        one[1].wait_recv()
        self.part[c, left, 0:half] = value[:half].astype(BF)
        self.part[c, left, half:GROUP] = (value[half:] + self.first[c, 1].astype(F32)).astype(BF)
        two[1].start()

    def own(self, c, product):
        value = product(c, self.at.y)
        for copy in self.twos(c):
            copy.wait_recv()
        self.part[c, self.at.y] = (
            value + self.second[c, 0].astype(F32) + self.second[c, 1].astype(F32)
        ).astype(BF)
        for copy in self.threes(c):
            copy.start()

    def result(self, c, rows):
        for copy in self.threes(c):
            copy.wait_recv()
        total = self.part[c, self.at.y, rows].astype(F32)
        for slot, _, _ in self.hand:
            total = total + self.third[c, slot].astype(F32)
        return total

    def drain(self, c):
        for copy in (*self.ones(c), *self.twos(c), *self.threes(c)):
            copy.wait_send()


class Gather:
    def __init__(self, at, mine, block, sems):
        self.at, self.mine, self.block = at, mine, block
        self.sems_line, self.sems_ring, self.sems_pass = sems

    def lines(self, c):
        return [
            send(self.mine(c), self.mine(c), self.sems_line, (c, k - 1), self.at.zdev(k))
            for k in (2, 1, 3)
        ]

    def rings(self, c):
        block = self.block(c, self.at.y, pl.ds(0, GROUP))
        return [
            send(block, block, self.sems_ring, (c, 0), self.at.ydev(1)),
            send(block, block, self.sems_ring, (c, 1), self.at.ydev(3)),
        ]

    def passes(self, c):
        low = self.block(c, self.at.yi(3), pl.ds(0, GROUP // 2))
        high = self.block(c, self.at.yi(1), pl.ds(GROUP // 2, GROUP // 2))
        return [
            send(low, low, self.sems_pass, (c, 0), self.at.ydev(1)),
            send(high, high, self.sems_pass, (c, 1), self.at.ydev(3)),
        ]

    def line(self, c):
        for copy in self.lines(c):
            copy.start()

    def arrived(self, c):
        for copy in self.lines(c):
            copy.wait_recv()

    def ring(self, c):
        for copy in self.rings(c):
            copy.start()

    def hand_on(self, c):
        for ring, onward in zip(self.rings(c), self.passes(c)):
            ring.wait_recv()
            onward.start()

    def finish(self, c):
        for copy in self.passes(c):
            copy.wait_recv()

    def drain(self, c):
        for copy in (*self.lines(c), *self.rings(c), *self.passes(c)):
            copy.wait_send()


class Squares:
    def __init__(self, at, part, near, mid, far, sems_y, sems_z):
        self.at, self.part, self.near, self.mid, self.far = at, part, near, mid, far
        self.sems_y, self.sems_z = sems_y, sems_z

    def fill(self, yy, wide):
        squared = (wide * wide).astype(BF)
        self.part[yy] = lax.dot_general(
            jnp.ones((8, wide.shape[1]), BF),
            squared,
            (((1,), (1,)), ((), ())),
            preferred_element_type=F32,
        )

    def ys(self):
        return [
            send(self.part.at[self.at.yi(k)], self.near.at[k - 1], self.sems_y, k - 1, self.at.ydev(k))
            for k in (1, 2, 3)
        ]

    def zs(self):
        return [
            send(self.mid, self.far.at[k - 1], self.sems_z, k - 1, self.at.zdev(k)) for k in (1, 2, 3)
        ]

    def start(self):
        for copy in self.ys():
            copy.start()

    def middle(self):
        for copy in self.ys():
            copy.wait_recv()
        self.mid[...] = self.part[self.at.y] + self.near[0] + self.near[1] + self.near[2]
        for copy in self.zs():
            copy.start()

    def scale(self, count, start):
        for copy in self.zs():
            copy.wait_recv()
        total = self.mid[...] + self.far[0] + self.far[1] + self.far[2]
        line = lax.rsqrt(total / WIDTH + EPS)[0:1]
        row = lax.broadcasted_iota(jnp.int32, (count, GROUP), 0)
        lane = lax.broadcasted_iota(jnp.int32, (count, GROUP), 1)
        picked = jnp.where(lane == row + start, jnp.broadcast_to(line, (count, GROUP)), 0.0)
        return jnp.sum(picked, axis=1, keepdims=True)

    def drain(self):
        for copy in (*self.ys(), *self.zs()):
            copy.wait_send()


def scaled(tokens, gain, out, squares, yy):
    wide = tokens[yy].astype(F32)
    squares.fill(yy, wide)
    out[yy] = (wide * gain).astype(BF)


def attention(at, m, gain, spread_weights):
    half = HEAD // 2
    lane = lax.broadcasted_iota(jnp.int32, (1, HEAD), 1)
    base = [m.table[i, pl.ds(ROWS + at.dp, 1), :] for i in range(2)]
    step = [m.table[i, 0:ROWS, :] for i in range(2)]
    cosine = base[0] * step[0] - base[1] * step[1]
    sine = (base[1] * step[0] + base[0] * step[1]) * jnp.where(lane < half, -1.0, 1.0)
    spread = Spread(at, m.tokens, m.gx)
    spread.start()
    spread.onward()
    spread.end()
    spread.finish()
    pending = spread.copies()

    squares = Squares(at, m.ss_part, m.ss_near, m.ss_mid, m.ss_far, m.ssy, m.ssz)
    along = [(k - 1, pl.ds(at.zi(k) * ROWS, ROWS), at.zdev(k)) for k in (2, 1, 3)]
    own_rows = pl.ds(at.z * ROWS, ROWS)
    qs = Reduce(at, m.q_part, m.q_one, m.q_two, m.q_three, (m.q1, m.q2, m.q3), along)
    q_chunks = m.q_part.shape[0]
    q_cols = m.q_part.shape[3]

    def product_q(c, yy):
        columns = m.wq[:, c * q_cols : (c + 1) * q_cols]
        return jnp.dot(m.normed[yy], columns, preferred_element_type=F32)

    def product_k(yy):
        return jnp.dot(m.normed[yy], m.wkv[...], preferred_element_type=F32)

    key_y = [
        send(m.k_part.at[at.yi(k)], m.k_near.at[k - 1], m.k1, k - 1, at.ydev(k)) for k in (2, 1, 3)
    ]
    for k, copy in zip((2, 1, 3), key_y):
        scaled(m.tokens, gain, m.normed, squares, at.yi(k))
        m.k_part[at.yi(k)] = product_k(at.yi(k)).astype(BF)
        copy.start()
    squares.start()
    for c in range(q_chunks):
        qs.far(c, product_q)
    scaled(m.tokens, gain, m.normed, squares, at.y)
    total = product_k(at.y)
    for k, copy in zip((2, 1, 3), key_y):
        copy.wait_recv()
        total = total + m.k_near[k - 1].astype(F32)
    m.k_part[at.y] = total.astype(BF)
    key_z = [
        send(m.k_part.at[at.y, rows], m.k_far.at[slot], m.k2, slot, device)
        for slot, rows, device in along
    ]
    for copy in key_z:
        copy.start()
    squares.middle()
    for c in range(q_chunks):
        qs.near(c, product_q)
    scale = squares.scale(ROWS, at.z * ROWS)

    def rotated(value, cos, sin):
        return value * cos + pltpu.roll(value, half, 1) * sin

    is_key = at.core == 0
    core = at.core
    value = m.k_part[at.y, own_rows].astype(F32)
    for slot, copy in zip((1, 0, 2), key_z):
        copy.wait_recv()
        value = value + m.k_far[slot].astype(F32)
    m.keys[core, at.y, own_rows] = rotated(
        value * scale, jnp.where(is_key, cosine, 1.0), jnp.where(is_key, sine, 0.0)
    ).astype(BF)
    mine = m.keys.at[core, at.y, own_rows]
    lines = [send(mine, mine, m.kl, k - 1, at.zdev(k)) for k in (2, 1, 3)]
    for copy in lines:
        copy.start()
    qs.own(0, product_q)
    for copy in lines:
        copy.wait_recv()
    block = m.keys.at[core, at.y]
    rings = [send(block, block, m.kr, k - 1, at.ydev(k)) for k in (2, 1, 3)]
    shares = [send(block, block, m.kc, 0, at.sibling())]
    for copy in rings + shares:
        copy.start()
    for c in range(1, q_chunks):
        qs.own(c, product_q)
    for k, ring in zip((2, 1, 3), rings):
        ring.wait_recv()
        came = m.keys.at[core, at.yi(RING - k)]
        shares.append(send(came, came, m.kc, k, at.sibling()))
        shares[-1].start()
    pending += key_y + key_z + lines + rings + shares

    per = q_cols // HEAD
    pieces = []
    for c in range(q_chunks):
        queries = qs.result(c, own_rows) * scale
        pieces += [rotated(queries[:, h * HEAD : (h + 1) * HEAD], cosine, sine) for h in range(per)]
    stacked = jnp.concatenate(pieces, axis=0).astype(BF)
    spread_weights(1)
    for copy in shares:
        copy.wait_recv()
    row = lax.broadcasted_iota(jnp.int32, (RING * ROWS, GROUP), 0)
    col = lax.broadcasted_iota(jnp.int32, (RING * ROWS, GROUP), 1)
    query_at = lax.rem(row, ROWS) + at.dp * ROWS
    key_at = lax.div(col, ROWS) * GROUP + lax.rem(col, ROWS)
    weight = jnp.zeros((RING * ROWS, 1), F32)
    for yy in range(RING):
        raw = lax.dot_general(
            stacked, m.keys[0, yy], (((1,), (1,)), ((), ())), preferred_element_type=F32
        ) * HEAD ** (-0.5)
        kept = jnp.where(key_at + yy * ROWS <= query_at, jnp.exp(raw), 0.0)
        m.scores[yy] = kept
        weight = weight + jnp.sum(kept, axis=1, keepdims=True)
    mix = jnp.zeros((RING * ROWS, HEAD), F32)
    for yy in range(RING):
        mix = mix + jnp.dot(
            (m.scores[yy] / weight).astype(BF), m.keys[1, yy], preferred_element_type=F32
        )

    def head_of(c):
        return pl.ds(c * HEAD, HEAD)

    heads = Gather(
        at,
        lambda c: m.mixed.at[at.y, own_rows, head_of(c)],
        lambda c, yy, rows: m.mixed.at[yy, rows, head_of(c)],
        (m.ml, m.mr, m.mp),
    )
    for h in range(RING):
        m.mixed[at.y, own_rows, h * HEAD : (h + 1) * HEAD] = mix[h * ROWS : (h + 1) * ROWS].astype(BF)
        heads.line(h)
    for h in range(RING):
        heads.arrived(h)
        heads.ring(h)
    spread_weights(2)
    for h in range(RING):
        heads.hand_on(h)

    def project(yy):
        m.a_part[yy] = jnp.dot(m.mixed[yy], m.wo[...], preferred_element_type=F32).astype(BF)

    project(at.y)
    project(at.yi(1))
    project(at.yi(3))
    for h in range(RING):
        heads.finish(h)
    project(at.yi(2))
    tile, more = scatter_x(at, m.a_part, m.a_pair, m.a_total, m.a_first, m.a_second, m.ax)

    def drain():
        for copy in pending + more:
            copy.wait_send()
        squares.drain()
        for c in range(q_chunks):
            qs.drain(c)
        for h in range(RING):
            heads.drain(h)

    return tile, drain


def kernel(names, *refs):
    m = types.SimpleNamespace()
    for name, ref in zip(names, refs):
        if name.endswith("_s"):
            setattr(m, name[:-2], [ref])
        elif name.endswith("_r"):
            getattr(m, name[:-2]).append(ref)
        else:
            setattr(m, name, ref)
    at = Place()
    chunks = m.wgu.shape[0]
    side, team = lax.rem(at.z, 2), lax.div(at.z, 2)
    partner = {"dp": (at.z + 1 - 2 * side) * RING + at.y}
    span = chunks * HEAD

    loads = [
        pltpu.make_async_copy(m.wq_hbm, m.wq, m.local.at[0]),
        pltpu.make_async_copy(
            m.wkv_hbm.at[at.core, :, pl.ds(at.x * HEAD, HEAD)], m.wkv, m.local.at[1]
        ),
        pltpu.make_async_copy(m.wo_hbm, m.wo, m.local.at[2]),
    ]

    def columns(n, c):
        return pl.ds(pl.multiple_of(n * span + c * HEAD, HEAD), HEAD)

    def kept(c, g):
        return pltpu.make_async_copy(
            m.wgu_hbm.at[g, :, columns(side, c)],
            m.wgu.at[c, side, :, pl.ds(g * HEAD, HEAD)],
            m.keep.at[c, g],
        )

    def given(c, g):
        return send(
            m.wgu_hbm.at[g, :, columns(1 - side, c)],
            m.wgu.at[c, side, :, pl.ds(g * HEAD, HEAD)],
            m.give,
            (c, g),
            partner,
        )

    def down(c, n):
        return pltpu.make_async_copy(
            m.wd_hbm.at[pl.ds(n * span + c * HEAD, HEAD)],
            m.wd.at[c, pl.ds(n * HEAD, HEAD)],
            m.down.at[c, n],
        )

    every = [(c, g) for c in range(chunks) for g in range(2)]
    shares = (every[:6], every[6:8], every[8:])

    def spread_weights(stage):
        for c, g in shares[stage]:
            given(c, g).start()

    for load in loads:
        load.start()
    enter(
        [at.ydev(k) for k in (1, 2, 3)]
        + [at.zdev(k) for k in (1, 2, 3)]
        + [at.xdev(1), at.xdev(3), at.sibling(), at.across()]
    )
    own = (pl.ds(2 * at.core, 2), pl.ds(at.x * ROWS, ROWS))
    swap = send(m.src, m.tokens.at[own], m.swap, 0, at.across())
    swap.start()
    for c, g in every:
        kept(c, g).start()
        down(c, g).start()
    for load in loads:
        load.wait()
    swap.wait_recv()
    spread_weights(0)
    tile, drain = attention(at, m, m.gain_attn[...].astype(F32), spread_weights)
    resid = (m.tokens[own].astype(F32) + tile).astype(BF)

    gain = m.gain_ffn[...].astype(F32)
    m.f_gained[...] = (resid.astype(F32) * gain[None]).astype(BF)
    trade = send(m.f_gained, m.f_tokens.at[(1, *own)], m.trade, 0, partner)
    trade.start()
    m.f_tokens[(0, *own)] = resid
    near, away = (Spread(at, m.f_tokens.at[i], sems) for i, sems in enumerate((m.fx, m.gz)))
    near.start()
    trade.wait_recv()
    away.start()
    near.onward()
    near.end()
    away.onward()
    away.end()
    near.finish()
    squares = Squares(at, m.fs_part, m.fs_near, m.fs_mid, m.fs_far, m.fsy, m.fsz)
    for k in (2, 1, 3):
        scaled(m.f_tokens.at[0], gain, m.f_normed, squares, at.yi(k))
    squares.start()
    scaled(m.f_tokens.at[0], gain, m.f_normed, squares, at.y)
    away.finish()

    fellow = [(0, pl.ds((1 - team) * 2 * ROWS, 2 * ROWS), at.zdev(2))]
    own_rows = pl.ds(team * 2 * ROWS, 2 * ROWS)
    own_lanes = pl.ds(pl.multiple_of(side * HEAD, HEAD), HEAD)
    hs = Reduce(at, m.h_part, m.h_one, m.h_two, m.h_three, (m.h1, m.h2, m.h3), fellow)
    hg = Gather(
        at,
        lambda c: m.hidden.at[c, at.y, own_rows, own_lanes],
        lambda c, yy, rows: m.hidden.at[c, yy, rows],
        (m.hl, m.hr, m.hp),
    )

    def product(c, yy):
        return jnp.dot(m.f_normed[yy], m.wgu[c, side], preferred_element_type=F32) + jnp.dot(
            m.f_tokens[1, yy], m.wgu[c, 1 - side], preferred_element_type=F32
        )

    def first(c):
        for g in range(2):
            kept(c, g).wait()
            given(c, g).wait_recv()
        hs.far(c, product)

    def activate(c):
        both = hs.result(c, own_rows) * m.scale[...]
        gate, up = both[:, :HEAD], both[:, HEAD:]
        m.hidden[c, at.y, own_rows, own_lanes] = (gate / (1.0 + jnp.exp(-gate)) * up).astype(BF)
        hg.line(c)

    def ring(c):
        hg.arrived(c)
        hg.ring(c)

    def add_down(c, k):
        yy = at.yi(k)
        m.acc[k] += jnp.dot(m.hidden[c, yy], m.wd[c], preferred_element_type=F32)

    def down_near(c):
        for n in range(2):
            down(c, n).wait()
        for k in (0, 1, 3):
            add_down(c, k)

    def down_far(c):
        hg.finish(c)
        add_down(c, 2)

    m.acc[...] = jnp.zeros_like(m.acc)
    squares.middle()
    m.scale[...] = jnp.broadcast_to(squares.scale(2 * ROWS, team * 2 * ROWS), m.scale.shape)
    stages = (
        (first, 0),
        (lambda c: hs.near(c, product), 2),
        (lambda c: hs.own(c, product), 4),
        (activate, 5),
        (ring, 6),
        (hg.hand_on, 7),
        (down_near, 8),
        (down_far, 9),
    )

    def turn(i, carry):
        for stage, lag in stages:
            c = i - lag

            @pl.when((c >= 0) & (c < chunks))
            def _():
                stage(c)

        return carry

    lax.fori_loop(0, chunks + stages[-1][1], turn, 0)
    for k in range(RING):
        m.f_part[at.yi(k)] = m.acc[k].astype(BF)
    tile, more = scatter_x(at, m.f_part, m.f_pair, m.f_total, m.f_first, m.f_second, m.bx)
    m.out[...] = (m.f_tokens[(0, *own)].astype(F32) + tile).astype(BF)

    def each(body):
        lax.fori_loop(0, chunks, lambda c, carry: (body(c), carry)[1], 0)

    drain()
    for copy in [swap, trade] + near.copies() + away.copies() + more:
        copy.wait_send()
    squares.drain()
    each(hs.drain)
    each(hg.drain)

    def drain_given(c):
        for g in range(2):
            given(c, g).wait_send()

    each(drain_given)


def reduce_scratch(name, chunks, columns, slots, rows):
    return {
        name + "_part": pltpu.VMEM((chunks, RING, GROUP, columns), BF),
        name + "_one": pltpu.VMEM((chunks, 2, GROUP // 2, columns), BF),
        name + "_two": pltpu.VMEM((chunks, 2, GROUP, columns), BF),
        name + "_three": pltpu.VMEM((chunks, slots, rows, columns), BF),
    }


def square_scratch(name):
    return {
        name + "_part": pltpu.VMEM((RING, 8, GROUP), F32),
        name + "_near": pltpu.VMEM((3, 8, GROUP), F32),
        name + "_mid": pltpu.VMEM((8, GROUP), F32),
        name + "_far": pltpu.VMEM((3, 8, GROUP), F32),
    }


def scatter_scratch(name, columns):
    return {
        name + "_part": pltpu.VMEM((RING, GROUP, columns), BF),
        name + "_pair": pltpu.VMEM((2, GROUP, columns), BF),
        name + "_total": pltpu.VMEM((2, GROUP, columns), BF),
        name + "_first": pltpu.VMEM((2, ROWS, columns), BF),
        name + "_second": pltpu.VMEM((2, 2, ROWS, columns), BF),
    }


def scratch(cols, heads, chunks, q_chunks):
    wide = 2 * HEAD
    buffers = {
        "tokens": pltpu.VMEM((RING, GROUP, cols), BF),
        "normed": pltpu.VMEM((RING, GROUP, cols), BF),
        "wq": pltpu.VMEM((cols, heads), BF),
        "wkv": pltpu.VMEM((cols, HEAD), BF),
        "wo": pltpu.VMEM((heads, cols), BF),
        **reduce_scratch("q", q_chunks, heads // q_chunks, 3, ROWS),
        "k_part": pltpu.VMEM((RING, GROUP, HEAD), BF),
        "k_near": pltpu.VMEM((3, GROUP, HEAD), BF),
        "k_far": pltpu.VMEM((3, ROWS, HEAD), BF),
        **square_scratch("ss"),
        "keys": pltpu.VMEM((2, RING, GROUP, HEAD), BF),
        "mixed": pltpu.VMEM((RING, GROUP, heads), BF),
        "scores": pltpu.VMEM((RING, RING * ROWS, GROUP), F32),
        **scatter_scratch("a", cols),
        "f_gained": pltpu.VMEM((2, ROWS, cols), BF),
        "f_tokens": pltpu.VMEM((2, RING, GROUP, cols), BF),
        "f_normed": pltpu.VMEM((RING, GROUP, cols), BF),
        "wgu": pltpu.VMEM((chunks, 2, cols, wide), BF),
        "wd": pltpu.VMEM((chunks, wide, cols), BF),
        **reduce_scratch("h", chunks, wide, 1, 2 * ROWS),
        **square_scratch("fs"),
        "scale": pltpu.VMEM((2 * ROWS, wide), F32),
        "hidden": pltpu.VMEM((chunks, RING, GROUP, wide), BF),
        "acc": pltpu.VMEM((RING, GROUP, cols), F32),
        **scatter_scratch("f", cols),
    }
    single = {"local": (3,), "keep": (chunks, 2), "down": (chunks, 2)}
    double = {
        "give": (chunks, 2), "swap": (1,), "trade": (1,),
        "gx": (8,), "fx": (8,), "gz": (8,), "ax": (8,), "bx": (8,),
        "ssy": (3,), "ssz": (3,), "fsy": (3,), "fsz": (3,),
        "q1": (q_chunks, 2), "q2": (q_chunks, 2), "q3": (q_chunks, 3),
        "k1": (3,), "k2": (3,), "kl": (3,), "kr": (3,), "kc": (4,),
        "ml": (RING, 3), "mr": (RING, 2), "mp": (RING, 2),
        "h1": (chunks, 2), "h2": (chunks, 2), "h3": (chunks, 1),
        "hl": (chunks, 3), "hr": (chunks, 2), "hp": (chunks, 2),
    }
    for name, shape in single.items():
        buffers[name] = pltpu.SemaphoreType.DMA(shape)
    for name, shape in double.items():
        buffers[name + "_s"] = pltpu.SemaphoreType.DMA(shape)
        buffers[name + "_r"] = pltpu.SemaphoreType.DMA(shape)
    return buffers


def rotary_table(count):
    freq = np.exp(-(2.0 * np.arange(HEAD // 2) / HEAD) * math.log(THETA))
    position = np.concatenate([np.arange(ROWS), np.arange(count) * ROWS]).astype(np.float64)
    angle = position[:, None] * np.concatenate([freq, freq])[None, :]
    return np.stack([np.cos(angle), np.sin(angle)]).astype(np.float32)


def local_layer(
    section_input, gain_attn, w_query, key_value_weight, w_output, gain_ffn, w_gate_up, w_down
):
    cols = section_input.shape[2]
    heads = w_query.shape[2]
    chunks = w_gate_up.shape[3] // (2 * HEAD)
    anywhere = pl.BlockSpec(memory_space=pl.ANY)
    vmem = pl.BlockSpec(memory_space=pltpu.VMEM)
    inputs = {
        "src": (section_input.reshape(2, ROWS, cols), anywhere),
        "gain_attn": (gain_attn, vmem),
        "wq_hbm": (w_query[0], anywhere),
        "wkv_hbm": (key_value_weight[0], anywhere),
        "wo_hbm": (w_output[0], anywhere),
        "gain_ffn": (gain_ffn, vmem),
        "wgu_hbm": (w_gate_up[0], anywhere),
        "wd_hbm": (w_down[0], anywhere),
        "table": (jnp.asarray(rotary_table(RING * RING)), vmem),
    }
    buffers = scratch(cols, heads, chunks, 2)
    result = pl.pallas_call(
        functools.partial(kernel, (*inputs, "out", *buffers)),
        name="layer",
        out_shape=jax.ShapeDtypeStruct((2, ROWS, cols), BF),
        in_specs=[spec for _, spec in inputs.values()],
        out_specs=vmem,
        scratch_shapes=list(buffers.values()),
        compiler_params=pltpu.CompilerParams(
            collective_id=0, has_side_effects=True, vmem_limit_bytes=60 * 1024 * 1024
        ),
    )(*[array for array, _ in inputs.values()])
    return result.reshape(1, 2 * ROWS, cols)


def solution(mesh):
    placed = (
        P("section", "tensor", "dp"),
        P("section", "dp"),
        P("section", "dp", "tensor"),
        P("section", None, "dp", None),
        P("section", "tensor", "dp"),
        P("section", "dp"),
        P("section", None, "dp", "tensor"),
        P("section", "tensor", "dp"),
    )
    return jax.shard_map(
        local_layer, mesh=mesh, in_specs=placed, out_specs=P("section", "tensor", "dp"), check_vma=False
    )
```

time: 220 us -> 179 us (0.81)
  Pallas kernels: 218 us -> 178 us
    pallas_call x2 -> x1, Pallas kernels: 218 us -> 178 us  [local_layer(): pl.pallas_call(functools.partial(kernel, (*inputs, 'out', *buffers)), nam...]
where the time goes in v2:
time: 179 us
  Pallas kernels  178 us (99%)
    pallas_call x1, Pallas kernels, local_layer(): pl.pallas_call(functools.partial(kernel, (*inputs, 'out', *buffers)), nam...  178 us

profile of v2, /device:TPU:1, one launch (start us, length us, event | category | flops | bytes accessed | tf_op | source)
XLA Modules:
  0.0 179.2 jit_solution(261130450694783405)
XLA Ops:
  0.0 177.6 %layer.1 = bf16[2,64,512]{2,1,0:T(8,128)(2,1)} custom-call(bf16[2,64,512]{2,1,0:T(8,128)(2,1)} %bitcast.13, bf16[1,512]{1,0:T(2,128)(2,1)} %refs_1_.1, bf16[512,512]{1,0:T(8,128)(2,1)} %bitcast.11, bf16[2,512,512]{2,1,0:T(8,128)(2,1)} %bitcast.9, bf16[512,512]{1,0:T(8,128)(2,1)} %bitcast.12, bf16[1,512]{1,0:T(2,128)(2,1)} %refs_5_.1, ...), custom_call_target="tpu_custom_call" | custom-call | tf_op jit(solution)/shard_map/layer/pallas_call | solution.py:805
  177.6 1.6 copy.11

commit v3 on v2

--- a/solution.py
+++ b/solution.py
@@ -17,6 +17,7 @@
 ROWS = 64
 GROUP = RING * ROWS
 WIDTH = 8192
+SPLIT = (5, 11)
 
 MESH_ID = pl.DeviceIdType.MESH
 BF = jnp.bfloat16
@@ -76,30 +77,30 @@
 
 
 class Spread:
-    def __init__(self, at, tokens, sems):
-        self.at = at
+    def __init__(self, at, tokens, h, sems):
         self.right, self.left, self.far = at.xi(1), at.xi(3), at.xi(2)
 
+        def rows(xx, start, count):
+            return tokens.at[2 * at.core + h, pl.ds(xx * ROWS + start, count)]
+
         def block(xx):
-            return tokens.at[pl.ds(2 * at.core, 2), pl.ds(xx * ROWS, ROWS)]
-
-        def half(xx, h):
-            return tokens.at[2 * at.core + h, pl.ds(xx * ROWS, ROWS)]
+            return rows(xx, 0, ROWS)
 
         def same(ref, index, device):
-            return send(ref, ref, sems, index, device)
-
+            return send(ref, ref, sems, (h, index), device)
+
+        half = ROWS // 2
         self.out = [
             same(block(at.x), 0, at.xdev(1)),
             same(block(at.x), 1, at.xdev(3)),
             same(block(at.x), 2, at.sibling()),
         ]
         self.after_left = [
-            same(half(self.left, 0), 3, at.xdev(1)),
+            same(rows(self.left, 0, half), 3, at.xdev(1)),
             same(block(self.left), 4, at.sibling()),
         ]
         self.after_right = [
-            same(half(self.right, 1), 5, at.xdev(3)),
+            same(rows(self.right, half, half), 5, at.xdev(3)),
             same(block(self.right), 6, at.sibling()),
         ]
         self.last = [same(block(self.far), 7, at.sibling())]
@@ -129,46 +130,67 @@
         return [*self.out, *self.after_left, *self.after_right, *self.last]
 
 
-def scatter_x(at, part, pair, total, first, second, sems):
-    mine, other = 2 * at.core, 2 * (1 - at.core)
-    right, left, far = at.xi(1), at.xi(3), at.xi(2)
-
-    def rows(xx):
+class Scatter:
+    def __init__(self, at, part, pair, total, first, second, h, sems):
+        self.at, self.part, self.pair, self.h = at, part, pair, h
+        self.total, self.first, self.second = total, first, second
+        self.mine, other = 2 * at.core + h, 2 * (1 - at.core) + h
+        self.right, self.left, self.far = at.xi(1), at.xi(3), at.xi(2)
+        self.half = ROWS // 2
+
+        def to(src, dst, index, device):
+            return send(src, dst, sems, (h, index), device)
+
+        self.shares = [
+            to(part.at[other, self.rows(xx)], pair.at[h, self.rows(xx)], i, at.sibling())
+            for i, xx in enumerate((self.far, self.right, self.left, at.x))
+        ]
+        self.ones = [
+            to(total.at[h, pl.ds(self.far * ROWS, self.half)], first.at[h, 0], 4, at.xdev(1)),
+            to(total.at[h, pl.ds(self.far * ROWS + self.half, self.half)], first.at[h, 1], 5, at.xdev(3)),
+        ]
+        self.twos = [
+            to(total.at[h, self.rows(self.right)], second.at[h, 0], 6, at.xdev(1)),
+            to(total.at[h, self.rows(self.left)], second.at[h, 1], 7, at.xdev(3)),
+        ]
+
+    def rows(self, xx):
         return pl.ds(xx * ROWS, ROWS)
 
-    shares = []
-    for i, xx in enumerate((far, right, left, at.x)):
-        shares.append(
-            send(part.at[pl.ds(other, 2), rows(xx)], pair.at[:, rows(xx)], sems, i, at.sibling())
-        )
-        shares[-1].start()
-
-    def summed(i, xx):
-        shares[i].wait_recv()
-        return part[pl.ds(mine, 2), rows(xx)].astype(F32) + pair[:, rows(xx)].astype(F32)
-
-    total[:, rows(far)] = summed(0, far).astype(BF)
-    one_right = send(total.at[0, rows(far)], first.at[0], sems, 4, at.xdev(1))
-    one_left = send(total.at[1, rows(far)], first.at[1], sems, 5, at.xdev(3))
-    one_right.start()
-    one_left.start()
-    to_right = summed(1, right)
-    one_right.wait_recv()
-    total[0, rows(right)] = (to_right[0] + first[0].astype(F32)).astype(BF)
-    total[1, rows(right)] = to_right[1].astype(BF)
-    two_right = send(total.at[:, rows(right)], second.at[0], sems, 6, at.xdev(1))
-    two_right.start()
-    to_left = summed(2, left)
-    one_left.wait_recv()
-    total[0, rows(left)] = to_left[0].astype(BF)
-    total[1, rows(left)] = (to_left[1] + first[1].astype(F32)).astype(BF)
-    two_left = send(total.at[:, rows(left)], second.at[1], sems, 7, at.xdev(3))
-    two_left.start()
-    own = summed(3, at.x)
-    two_right.wait_recv()
-    two_left.wait_recv()
-    tile = own + second[0].astype(F32) + second[1].astype(F32)
-    return tile, shares + [one_right, one_left, two_right, two_left]
+    def summed(self, i, xx):
+        self.shares[i].wait_recv()
+        return self.part[self.mine, self.rows(xx)].astype(F32) + self.pair[self.h, self.rows(xx)].astype(F32)
+
+    def start(self):
+        for copy in self.shares:
+            copy.start()
+
+    def step_one(self):
+        self.total[self.h, self.rows(self.far)] = self.summed(0, self.far).astype(BF)
+        for copy in self.ones:
+            copy.start()
+
+    def step_two(self):
+        half = self.half
+        value = self.summed(1, self.right)
+        self.ones[0].wait_recv()
+        added = value[:half] + self.first[self.h, 0].astype(F32)
+        self.total[self.h, self.rows(self.right)] = jnp.concatenate([added, value[half:]], axis=0).astype(BF)
+        self.twos[0].start()
+        value = self.summed(2, self.left)
+        self.ones[1].wait_recv()
+        added = value[half:] + self.first[self.h, 1].astype(F32)
+        self.total[self.h, self.rows(self.left)] = jnp.concatenate([value[:half], added], axis=0).astype(BF)
+        self.twos[1].start()
+
+    def result(self):
+        own = self.summed(3, self.at.x)
+        for copy in self.twos:
+            copy.wait_recv()
+        return own + self.second[self.h, 0].astype(F32) + self.second[self.h, 1].astype(F32)
+
+    def copies(self):
+        return [*self.shares, *self.ones, *self.twos]
 
 
 class Reduce:
@@ -352,19 +374,20 @@
     out[yy] = (wide * gain).astype(BF)
 
 
-def attention(at, m, gain, spread_weights):
+def attention(at, m, spread, gain, spread_weights):
     half = HEAD // 2
     lane = lax.broadcasted_iota(jnp.int32, (1, HEAD), 1)
     base = [m.table[i, pl.ds(ROWS + at.dp, 1), :] for i in range(2)]
     step = [m.table[i, 0:ROWS, :] for i in range(2)]
     cosine = base[0] * step[0] - base[1] * step[1]
     sine = (base[1] * step[0] + base[0] * step[1]) * jnp.where(lane < half, -1.0, 1.0)
-    spread = Spread(at, m.tokens, m.gx)
-    spread.start()
-    spread.onward()
-    spread.end()
-    spread.finish()
-    pending = spread.copies()
+    for piece in spread:
+        piece.onward()
+    for piece in spread:
+        piece.end()
+    for piece in spread:
+        piece.finish()
+    pending = [copy for piece in spread for copy in piece.copies()]
 
     squares = Squares(at, m.ss_part, m.ss_near, m.ss_mid, m.ss_far, m.ssy, m.ssz)
     along = [(k - 1, pl.ds(at.zi(k) * ROWS, ROWS), at.zdev(k)) for k in (2, 1, 3)]
@@ -446,7 +469,6 @@
         queries = qs.result(c, own_rows) * scale
         pieces += [rotated(queries[:, h * HEAD : (h + 1) * HEAD], cosine, sine) for h in range(per)]
     stacked = jnp.concatenate(pieces, axis=0).astype(BF)
-    spread_weights(1)
     for copy in shares:
         copy.wait_recv()
     row = lax.broadcasted_iota(jnp.int32, (RING * ROWS, GROUP), 0)
@@ -482,7 +504,7 @@
     for h in range(RING):
         heads.arrived(h)
         heads.ring(h)
-    spread_weights(2)
+    spread_weights(1)
     for h in range(RING):
         heads.hand_on(h)
 
@@ -495,10 +517,9 @@
     for h in range(RING):
         heads.finish(h)
     project(at.yi(2))
-    tile, more = scatter_x(at, m.a_part, m.a_pair, m.a_total, m.a_first, m.a_second, m.ax)
 
     def drain():
-        for copy in pending + more:
+        for copy in pending:
             copy.wait_send()
         squares.drain()
         for c in range(q_chunks):
@@ -506,7 +527,7 @@
         for h in range(RING):
             heads.drain(h)
 
-    return tile, drain
+    return drain
 
 
 def kernel(names, *refs):
@@ -524,13 +545,30 @@
     partner = {"dp": (at.z + 1 - 2 * side) * RING + at.y}
     span = chunks * HEAD
 
+    enter(
+        [at.ydev(k) for k in (1, 2, 3)]
+        + [at.zdev(k) for k in (1, 2, 3)]
+        + [at.xdev(1), at.xdev(3), at.sibling(), at.across()]
+    )
+    own = [(2 * at.core + h, pl.ds(at.x * ROWS, ROWS)) for h in range(2)]
+    swaps = [send(m.src.at[h], m.tokens.at[own[h]], m.swap, h, at.across()) for h in range(2)]
+    for swap in swaps:
+        swap.start()
     loads = [
-        pltpu.make_async_copy(m.wq_hbm, m.wq, m.local.at[0]),
-        pltpu.make_async_copy(
-            m.wkv_hbm.at[at.core, :, pl.ds(at.x * HEAD, HEAD)], m.wkv, m.local.at[1]
-        ),
-        pltpu.make_async_copy(m.wo_hbm, m.wo, m.local.at[2]),
+        pltpu.make_async_copy(*pair, m.local.at[i])
+        for i, pair in enumerate(
+            (
+                (m.gain_attn_hbm, m.gain_attn),
+                (m.wkv_hbm.at[at.core, :, pl.ds(at.x * HEAD, HEAD)], m.wkv),
+                (m.wq_hbm, m.wq),
+                (m.table_hbm, m.table),
+                (m.wo_hbm, m.wo),
+                (m.gain_ffn_hbm, m.gain_ffn),
+            )
+        )
     ]
+    for load in loads:
+        load.start()
 
     def columns(n, c):
         return pl.ds(pl.multiple_of(n * span + c * HEAD, HEAD), HEAD)
@@ -559,52 +597,68 @@
         )
 
     every = [(c, g) for c in range(chunks) for g in range(2)]
-    shares = (every[:6], every[6:8], every[8:])
+    shares = (every[:SPLIT[0]], every[SPLIT[0]:SPLIT[1]], every[SPLIT[1]:])
 
     def spread_weights(stage):
         for c, g in shares[stage]:
             given(c, g).start()
 
-    for load in loads:
-        load.start()
-    enter(
-        [at.ydev(k) for k in (1, 2, 3)]
-        + [at.zdev(k) for k in (1, 2, 3)]
-        + [at.xdev(1), at.xdev(3), at.sibling(), at.across()]
-    )
-    own = (pl.ds(2 * at.core, 2), pl.ds(at.x * ROWS, ROWS))
-    swap = send(m.src, m.tokens.at[own], m.swap, 0, at.across())
-    swap.start()
     for c, g in every:
         kept(c, g).start()
         down(c, g).start()
     for load in loads:
         load.wait()
-    swap.wait_recv()
+    spread = [Spread(at, m.tokens, h, m.gx) for h in range(2)]
+    for swap, piece in zip(swaps, spread):
+        swap.wait_recv()
+        piece.start()
     spread_weights(0)
-    tile, drain = attention(at, m, m.gain_attn[...].astype(F32), spread_weights)
-    resid = (m.tokens[own].astype(F32) + tile).astype(BF)
+    drain = attention(at, m, spread, m.gain_attn[...].astype(F32), spread_weights)
+
+    def scatters(part, pair, total, first, second, sems):
+        pieces = [Scatter(at, part, pair, total, first, second, h, sems) for h in range(2)]
+        for piece in pieces:
+            piece.start()
+        for piece in pieces:
+            piece.step_one()
+        for piece in pieces:
+            piece.step_two()
+        return pieces
 
     gain = m.gain_ffn[...].astype(F32)
-    m.f_gained[...] = (resid.astype(F32) * gain[None]).astype(BF)
-    trade = send(m.f_gained, m.f_tokens.at[(1, *own)], m.trade, 0, partner)
-    trade.start()
-    m.f_tokens[(0, *own)] = resid
-    near, away = (Spread(at, m.f_tokens.at[i], sems) for i, sems in enumerate((m.fx, m.gz)))
-    near.start()
-    trade.wait_recv()
-    away.start()
-    near.onward()
-    near.end()
-    away.onward()
-    away.end()
-    near.finish()
+    scatter_a = scatters(m.a_part, m.a_pair, m.a_total, m.a_first, m.a_second, m.ax)
+    trades = [
+        send(m.f_gained.at[h], m.f_tokens.at[(1, *own[h])], m.trade, h, partner) for h in range(2)
+    ]
+    near, away = (
+        [Spread(at, m.f_tokens.at[i], h, sems) for h in range(2)] for i, sems in enumerate((m.fx, m.gz))
+    )
+    for h in range(2):
+        resid = (m.tokens[own[h]].astype(F32) + scatter_a[h].result()).astype(BF)
+        m.f_gained[h] = (resid.astype(F32) * gain).astype(BF)
+        trades[h].start()
+        m.f_tokens[(0, *own[h])] = resid
+        near[h].start()
+    spread_weights(2)
+    for h in range(2):
+        trades[h].wait_recv()
+        away[h].start()
+        near[h].onward()
+    for h in range(2):
+        near[h].end()
+        away[h].onward()
+    for h in range(2):
+        away[h].end()
+    for h in range(2):
+        near[h].finish()
     squares = Squares(at, m.fs_part, m.fs_near, m.fs_mid, m.fs_far, m.fsy, m.fsz)
     for k in (2, 1, 3):
         scaled(m.f_tokens.at[0], gain, m.f_normed, squares, at.yi(k))
     squares.start()
     scaled(m.f_tokens.at[0], gain, m.f_normed, squares, at.y)
-    away.finish()
+    m.acc[...] = jnp.zeros_like(m.acc)
+    for h in range(2):
+        away[h].finish()
 
     fellow = [(0, pl.ds((1 - team) * 2 * ROWS, 2 * ROWS), at.zdev(2))]
     own_rows = pl.ds(team * 2 * ROWS, 2 * ROWS)
@@ -652,7 +706,6 @@
         hg.finish(c)
         add_down(c, 2)
 
-    m.acc[...] = jnp.zeros_like(m.acc)
     squares.middle()
     m.scale[...] = jnp.broadcast_to(squares.scale(2 * ROWS, team * 2 * ROWS), m.scale.shape)
     stages = (
@@ -679,15 +732,19 @@
     lax.fori_loop(0, chunks + stages[-1][1], turn, 0)
     for k in range(RING):
         m.f_part[at.yi(k)] = m.acc[k].astype(BF)
-    tile, more = scatter_x(at, m.f_part, m.f_pair, m.f_total, m.f_first, m.f_second, m.bx)
-    m.out[...] = (m.f_tokens[(0, *own)].astype(F32) + tile).astype(BF)
+    scatter_f = scatters(m.f_part, m.f_pair, m.f_total, m.f_first, m.f_second, m.bx)
+    for h in range(2):
+        m.out[h] = (m.f_tokens[(0, *own[h])].astype(F32) + scatter_f[h].result()).astype(BF)
 
     def each(body):
         lax.fori_loop(0, chunks, lambda c, carry: (body(c), carry)[1], 0)
 
     drain()
-    for copy in [swap, trade] + near.copies() + away.copies() + more:
+    for copy in swaps + trades:
         copy.wait_send()
+    for piece in near + away + scatter_a + scatter_f:
+        for copy in piece.copies():
+            copy.wait_send()
     squares.drain()
     each(hs.drain)
     each(hg.drain)
@@ -722,7 +779,7 @@
         name + "_part": pltpu.VMEM((RING, GROUP, columns), BF),
         name + "_pair": pltpu.VMEM((2, GROUP, columns), BF),
         name + "_total": pltpu.VMEM((2, GROUP, columns), BF),
-        name + "_first": pltpu.VMEM((2, ROWS, columns), BF),
+        name + "_first": pltpu.VMEM((2, 2, ROWS // 2, columns), BF),
         name + "_second": pltpu.VMEM((2, 2, ROWS, columns), BF),
     }
 
@@ -730,6 +787,9 @@
 def scratch(cols, heads, chunks, q_chunks):
     wide = 2 * HEAD
     buffers = {
+        "gain_attn": pltpu.VMEM((1, cols), BF),
+        "gain_ffn": pltpu.VMEM((1, cols), BF),
+        "table": pltpu.VMEM((2, ROWS + RING * RING, HEAD), F32),
         "tokens": pltpu.VMEM((RING, GROUP, cols), BF),
         "normed": pltpu.VMEM((RING, GROUP, cols), BF),
         "wq": pltpu.VMEM((cols, heads), BF),
@@ -756,10 +816,10 @@
         "acc": pltpu.VMEM((RING, GROUP, cols), F32),
         **scatter_scratch("f", cols),
     }
-    single = {"local": (3,), "keep": (chunks, 2), "down": (chunks, 2)}
+    single = {"local": (6,), "keep": (chunks, 2), "down": (chunks, 2)}
     double = {
-        "give": (chunks, 2), "swap": (1,), "trade": (1,),
-        "gx": (8,), "fx": (8,), "gz": (8,), "ax": (8,), "bx": (8,),
+        "give": (chunks, 2), "swap": (2,), "trade": (2,),
+        "gx": (2, 8), "fx": (2, 8), "gz": (2, 8), "ax": (2, 8), "bx": (2, 8),
         "ssy": (3,), "ssz": (3,), "fsy": (3,), "fsz": (3,),
         "q1": (q_chunks, 2), "q2": (q_chunks, 2), "q3": (q_chunks, 3),
         "k1": (3,), "k2": (3,), "kl": (3,), "kr": (3,), "kc": (4,),
@@ -792,14 +852,14 @@
     vmem = pl.BlockSpec(memory_space=pltpu.VMEM)
     inputs = {
         "src": (section_input.reshape(2, ROWS, cols), anywhere),
-        "gain_attn": (gain_attn, vmem),
+        "gain_attn_hbm": (gain_attn, anywhere),
         "wq_hbm": (w_query[0], anywhere),
         "wkv_hbm": (key_value_weight[0], anywhere),
         "wo_hbm": (w_output[0], anywhere),
-        "gain_ffn": (gain_ffn, vmem),
+        "gain_ffn_hbm": (gain_ffn, anywhere),
         "wgu_hbm": (w_gate_up[0], anywhere),
         "wd_hbm": (w_down[0], anywhere),
-        "table": (jnp.asarray(rotary_table(RING * RING)), vmem),
+        "table_hbm": (jnp.asarray(rotary_table(RING * RING)), anywhere),
     }
     buffers = scratch(cols, heads, chunks, 2)
     result = pl.pallas_call(

time: 179 us -> 171 us (0.955)
  Pallas kernels: 178 us -> 169 us
    pallas_call x1, Pallas kernels: 178 us -> 169 us  [local_layer(): pl.pallas_call(functools.partial(kernel, (*inputs, 'out', *buffers)), nam...]
where the time goes in v3:
time: 171 us
  Pallas kernels  169 us (99%)
    pallas_call x1, Pallas kernels, local_layer(): pl.pallas_call(functools.partial(kernel, (*inputs, 'out', *buffers)), nam...  169 us

profile of v3, /device:TPU:1, one launch (start us, length us, event | category | flops | bytes accessed | tf_op | source)
XLA Modules:
  0.0 170.6 jit_solution(14635889642410438110)
XLA Ops:
  0.0 169.1 %layer.1 = bf16[2,64,512]{2,1,0:T(8,128)(2,1)} custom-call(bf16[2,64,512]{2,1,0:T(8,128)(2,1)} %bitcast.13, bf16[1,512]{1,0:T(2,128)(2,1)} %refs_1_.1, bf16[512,512]{1,0:T(8,128)(2,1)} %bitcast.11, bf16[2,512,512]{2,1,0:T(8,128)(2,1)} %bitcast.9, bf16[512,512]{1,0:T(8,128)(2,1)} %bitcast.12, bf16[1,512]{1,0:T(2,128)(2,1)} %refs_5_.1, ...), custom_call_target="tpu_custom_call" | custom-call | tf_op jit(solution)/shard_map/layer/pallas_call | solution.py:865
  169.1 1.6 copy.11

commit v4 on v3

--- a/solution.py
+++ b/solution.py
@@ -17,7 +17,7 @@
 ROWS = 64
 GROUP = RING * ROWS
 WIDTH = 8192
-SPLIT = (5, 11)
+SPLIT = (5, 10)
 
 MESH_ID = pl.DeviceIdType.MESH
 BF = jnp.bfloat16
@@ -271,10 +271,7 @@
         self.sems_line, self.sems_ring, self.sems_pass = sems
 
     def lines(self, c):
-        return [
-            send(self.mine(c), self.mine(c), self.sems_line, (c, k - 1), self.at.zdev(k))
-            for k in (2, 1, 3)
-        ]
+        return [send(self.mine(c), self.mine(c), self.sems_line, c, self.at.zdev(2))]
 
     def rings(self, c):
         block = self.block(c, self.at.y, pl.ds(0, GROUP))
@@ -489,24 +486,40 @@
             (m.scores[yy] / weight).astype(BF), m.keys[1, yy], preferred_element_type=F32
         )
 
-    def head_of(c):
-        return pl.ds(c * HEAD, HEAD)
-
-    heads = Gather(
-        at,
-        lambda c: m.mixed.at[at.y, own_rows, head_of(c)],
-        lambda c, yy, rows: m.mixed.at[yy, rows, head_of(c)],
-        (m.ml, m.mr, m.mp),
-    )
+    def rows_of(yy, k, start=0, count=ROWS):
+        return m.mixed.at[yy, pl.ds(at.zi(k) * ROWS + start, count)]
+
+    def rings_of(k):
+        block = rows_of(at.y, k)
+        return [send(block, block, m.mr, (k, i), at.ydev(way)) for i, way in enumerate((1, 3))]
+
+    def passes_of(k):
+        low, high = rows_of(at.yi(3), k, 0, ROWS // 2), rows_of(at.yi(1), k, ROWS // 2, ROWS // 2)
+        return [send(low, low, m.mp, (k, 0), at.ydev(1)), send(high, high, m.mp, (k, 1), at.ydev(3))]
+
+    def ring(k):
+        for copy in rings_of(k):
+            copy.start()
+
+    def hand_on(k):
+        for came, onward in zip(rings_of(k), passes_of(k)):
+            came.wait_recv()
+            onward.start()
+
     for h in range(RING):
         m.mixed[at.y, own_rows, h * HEAD : (h + 1) * HEAD] = mix[h * ROWS : (h + 1) * ROWS].astype(BF)
-        heads.line(h)
-    for h in range(RING):
-        heads.arrived(h)
-        heads.ring(h)
+    lines_m = {k: send(rows_of(at.y, 0), rows_of(at.y, 0), m.ml, k - 1, at.zdev(k)) for k in (1, 3, 2)}
+    for copy in lines_m.values():
+        copy.start()
+    ring(0)
+    before = 0
+    for k in (1, 3, 2):
+        lines_m[RING - k].wait_recv()
+        ring(k)
+        hand_on(before)
+        before = k
     spread_weights(1)
-    for h in range(RING):
-        heads.hand_on(h)
+    hand_on(before)
 
     def project(yy):
         m.a_part[yy] = jnp.dot(m.mixed[yy], m.wo[...], preferred_element_type=F32).astype(BF)
@@ -514,18 +527,20 @@
     project(at.y)
     project(at.yi(1))
     project(at.yi(3))
-    for h in range(RING):
-        heads.finish(h)
+    for k in range(RING):
+        for copy in passes_of(k):
+            copy.wait_recv()
     project(at.yi(2))
 
     def drain():
-        for copy in pending:
+        for copy in pending + list(lines_m.values()):
             copy.wait_send()
         squares.drain()
         for c in range(q_chunks):
             qs.drain(c)
-        for h in range(RING):
-            heads.drain(h)
+        for k in range(RING):
+            for copy in (*rings_of(k), *passes_of(k)):
+                copy.wait_send()
 
     return drain
 
@@ -589,11 +604,14 @@
             partner,
         )
 
-    def down(c, n):
+    def down(c):
         return pltpu.make_async_copy(
-            m.wd_hbm.at[pl.ds(n * span + c * HEAD, HEAD)],
-            m.wd.at[c, pl.ds(n * HEAD, HEAD)],
-            m.down.at[c, n],
+            m.wd_hbm.at[pl.ds(side * span + c * HEAD, HEAD)], m.wd.at[c, side], m.down.at[c]
+        )
+
+    def lent(c):
+        return send(
+            m.wd_hbm.at[pl.ds((1 - side) * span + c * HEAD, HEAD)], m.wd.at[c, side], m.lend, c, partner
         )
 
     every = [(c, g) for c in range(chunks) for g in range(2)]
@@ -605,7 +623,8 @@
 
     for c, g in every:
         kept(c, g).start()
-        down(c, g).start()
+    for c in range(chunks):
+        down(c).start()
     for load in loads:
         load.wait()
     spread = [Spread(at, m.tokens, h, m.gx) for h in range(2)]
@@ -662,11 +681,10 @@
 
     fellow = [(0, pl.ds((1 - team) * 2 * ROWS, 2 * ROWS), at.zdev(2))]
     own_rows = pl.ds(team * 2 * ROWS, 2 * ROWS)
-    own_lanes = pl.ds(pl.multiple_of(side * HEAD, HEAD), HEAD)
     hs = Reduce(at, m.h_part, m.h_one, m.h_two, m.h_three, (m.h1, m.h2, m.h3), fellow)
     hg = Gather(
         at,
-        lambda c: m.hidden.at[c, at.y, own_rows, own_lanes],
+        lambda c: m.hidden.at[c, at.y, own_rows],
         lambda c, yy, rows: m.hidden.at[c, yy, rows],
         (m.hl, m.hr, m.hp),
     )
@@ -681,11 +699,12 @@
             kept(c, g).wait()
             given(c, g).wait_recv()
         hs.far(c, product)
+        lent(c).start()
 
     def activate(c):
         both = hs.result(c, own_rows) * m.scale[...]
         gate, up = both[:, :HEAD], both[:, HEAD:]
-        m.hidden[c, at.y, own_rows, own_lanes] = (gate / (1.0 + jnp.exp(-gate)) * up).astype(BF)
+        m.hidden[c, at.y, own_rows] = (gate / (1.0 + jnp.exp(-gate)) * up).astype(BF)
         hg.line(c)
 
     def ring(c):
@@ -694,11 +713,12 @@
 
     def add_down(c, k):
         yy = at.yi(k)
-        m.acc[k] += jnp.dot(m.hidden[c, yy], m.wd[c], preferred_element_type=F32)
+        m.acc[0, k] += jnp.dot(m.hidden[c, yy], m.wd[c, side], preferred_element_type=F32)
+        m.acc[1, k] += jnp.dot(m.hidden[c, yy], m.wd[c, 1 - side], preferred_element_type=F32)
 
     def down_near(c):
-        for n in range(2):
-            down(c, n).wait()
+        down(c).wait()
+        lent(c).wait_recv()
         for k in (0, 1, 3):
             add_down(c, k)
 
@@ -706,8 +726,11 @@
         hg.finish(c)
         add_down(c, 2)
 
-    squares.middle()
-    m.scale[...] = jnp.broadcast_to(squares.scale(2 * ROWS, team * 2 * ROWS), m.scale.shape)
+
+    def row_scale():
+        m.scale[...] = jnp.broadcast_to(squares.scale(2 * ROWS, team * 2 * ROWS), m.scale.shape)
+
+    once = ((squares.middle, 2), (row_scale, 4))
     stages = (
         (first, 0),
         (lambda c: hs.near(c, product), 2),
@@ -720,6 +743,8 @@
     )
 
     def turn(i, carry):
+        for step, when in once:
+            pl.when(i == when)(step)
         for stage, lag in stages:
             c = i - lag
 
@@ -730,19 +755,42 @@
         return carry
 
     lax.fori_loop(0, chunks + stages[-1][1], turn, 0)
-    for k in range(RING):
-        m.f_part[at.yi(k)] = m.acc[k].astype(BF)
-    scatter_f = scatters(m.f_part, m.f_pair, m.f_total, m.f_first, m.f_second, m.bx)
+    others = [
+        Scatter(at, m.g_part, m.g_pair, m.g_total, m.g_first, m.g_second, h, m.cx) for h in range(2)
+    ]
+    owns = [
+        Scatter(at, m.f_part, m.f_pair, m.f_total, m.f_first, m.f_second, h, m.bx) for h in range(2)
+    ]
+    for j, part, pieces in ((1, m.g_part, others), (0, m.f_part, owns)):
+        for yy, piece in zip((2 * (1 - at.core), 2 * (1 - at.core) + 1), pieces):
+            part[yy] = m.acc[j, lax.rem(yy - at.y + RING, RING)].astype(BF)
+            piece.start()
+        for yy in (2 * at.core, 2 * at.core + 1):
+            part[yy] = m.acc[j, lax.rem(yy - at.y + RING, RING)].astype(BF)
+    for piece in others:
+        piece.step_one()
+    for piece in owns:
+        piece.step_one()
+    for piece in others:
+        piece.step_two()
+    for piece in owns:
+        piece.step_two()
+    backs = [send(m.back_out.at[h], m.back_in.at[h], m.back, h, partner) for h in range(2)]
     for h in range(2):
-        m.out[h] = (m.f_tokens[(0, *own[h])].astype(F32) + scatter_f[h].result()).astype(BF)
+        m.back_out[h] = others[h].result().astype(BF)
+        backs[h].start()
+    for h in range(2):
+        value = m.f_tokens[(0, *own[h])].astype(F32) + owns[h].result()
+        backs[h].wait_recv()
+        m.out[h] = (value + m.back_in[h].astype(F32)).astype(BF)
 
     def each(body):
         lax.fori_loop(0, chunks, lambda c, carry: (body(c), carry)[1], 0)
 
     drain()
-    for copy in swaps + trades:
+    for copy in swaps + trades + backs:
         copy.wait_send()
-    for piece in near + away + scatter_a + scatter_f:
+    for piece in near + away + scatter_a + others + owns:
         for copy in piece.copies():
             copy.wait_send()
     squares.drain()
@@ -752,6 +800,7 @@
     def drain_given(c):
         for g in range(2):
             given(c, g).wait_send()
+        lent(c).wait_send()
 
     each(drain_given)
 
@@ -808,24 +857,27 @@
         "f_tokens": pltpu.VMEM((2, RING, GROUP, cols), BF),
         "f_normed": pltpu.VMEM((RING, GROUP, cols), BF),
         "wgu": pltpu.VMEM((chunks, 2, cols, wide), BF),
-        "wd": pltpu.VMEM((chunks, wide, cols), BF),
+        "wd": pltpu.VMEM((chunks, 2, HEAD, cols), BF),
         **reduce_scratch("h", chunks, wide, 1, 2 * ROWS),
         **square_scratch("fs"),
         "scale": pltpu.VMEM((2 * ROWS, wide), F32),
-        "hidden": pltpu.VMEM((chunks, RING, GROUP, wide), BF),
-        "acc": pltpu.VMEM((RING, GROUP, cols), F32),
+        "hidden": pltpu.VMEM((chunks, RING, GROUP, HEAD), BF),
+        "acc": pltpu.VMEM((2, RING, GROUP, cols), F32),
         **scatter_scratch("f", cols),
+        **scatter_scratch("g", cols),
+        "back_out": pltpu.VMEM((2, ROWS, cols), BF),
+        "back_in": pltpu.VMEM((2, ROWS, cols), BF),
     }
-    single = {"local": (6,), "keep": (chunks, 2), "down": (chunks, 2)}
+    single = {"local": (6,), "keep": (chunks, 2), "down": (chunks,)}
     double = {
-        "give": (chunks, 2), "swap": (2,), "trade": (2,),
+        "give": (chunks, 2), "lend": (chunks,), "back": (2,), "cx": (2, 8), "swap": (2,), "trade": (2,),
         "gx": (2, 8), "fx": (2, 8), "gz": (2, 8), "ax": (2, 8), "bx": (2, 8),
         "ssy": (3,), "ssz": (3,), "fsy": (3,), "fsz": (3,),
         "q1": (q_chunks, 2), "q2": (q_chunks, 2), "q3": (q_chunks, 3),
         "k1": (3,), "k2": (3,), "kl": (3,), "kr": (3,), "kc": (4,),
-        "ml": (RING, 3), "mr": (RING, 2), "mp": (RING, 2),
+        "ml": (3,), "mr": (RING, 2), "mp": (RING, 2),
         "h1": (chunks, 2), "h2": (chunks, 2), "h3": (chunks, 1),
-        "hl": (chunks, 3), "hr": (chunks, 2), "hp": (chunks, 2),
+        "hl": (chunks,), "hr": (chunks, 2), "hp": (chunks, 2),
     }
     for name, shape in single.items():
         buffers[name] = pltpu.SemaphoreType.DMA(shape)

time: 171 us -> 165 us (0.965)
  Pallas kernels: 169 us -> 163 us
    pallas_call x1, Pallas kernels: 169 us -> 163 us  [local_layer(): pl.pallas_call(functools.partial(kernel, (*inputs, 'out', *buffers)), nam...]
where the time goes in v4:
time: 165 us
  Pallas kernels  163 us (99%)
    pallas_call x1, Pallas kernels, local_layer(): pl.pallas_call(functools.partial(kernel, (*inputs, 'out', *buffers)), nam...  163 us

profile of v4, /device:TPU:1, one launch (start us, length us, event | category | flops | bytes accessed | tf_op | source)
XLA Modules:
  0.0 164.5 jit_solution(1789532966291993600)
XLA Ops:
  0.0 162.9 %layer.1 = bf16[2,64,512]{2,1,0:T(8,128)(2,1)} custom-call(bf16[2,64,512]{2,1,0:T(8,128)(2,1)} %bitcast.13, bf16[1,512]{1,0:T(2,128)(2,1)} %refs_1_.1, bf16[512,512]{1,0:T(8,128)(2,1)} %bitcast.11, bf16[2,512,512]{2,1,0:T(8,128)(2,1)} %bitcast.9, bf16[512,512]{1,0:T(8,128)(2,1)} %bitcast.12, bf16[1,512]{1,0:T(2,128)(2,1)} %refs_5_.1, ...), custom_call_target="tpu_custom_call" | custom-call | tf_op jit(solution)/shard_map/layer/pallas_call | solution.py:917
  163.0 1.6 copy.11

commit v5 on v4

--- a/solution.py
+++ b/solution.py
@@ -711,21 +711,34 @@
         hg.arrived(c)
         hg.ring(c)
 
-    def add_down(c, k):
+    def add_down(held, k):
         yy = at.yi(k)
-        m.acc[0, k] += jnp.dot(m.hidden[c, yy], m.wd[c, side], preferred_element_type=F32)
-        m.acc[1, k] += jnp.dot(m.hidden[c, yy], m.wd[c, 1 - side], preferred_element_type=F32)
+        left = jnp.concatenate([m.hidden[c, yy] for c in held], axis=1)
+        for j, half in enumerate((side, 1 - side)):
+            right = jnp.concatenate([m.wd[c, half] for c in held], axis=0)
+            m.acc[j, k] += jnp.dot(left, right, preferred_element_type=F32)
+
+    def by_pairs(c, blocks):
+        @pl.when(lax.rem(c, 2) == 1)
+        def _():
+            for k in blocks:
+                add_down((c - 1, c), k)
+
+        if chunks % 2:
+
+            @pl.when(c == chunks - 1)
+            def _():
+                for k in blocks:
+                    add_down((c,), k)
 
     def down_near(c):
         down(c).wait()
         lent(c).wait_recv()
-        for k in (0, 1, 3):
-            add_down(c, k)
+        by_pairs(c, (0, 1, 3))
 
     def down_far(c):
         hg.finish(c)
-        add_down(c, 2)
-
+        by_pairs(c, (2,))
 
     def row_scale():
         m.scale[...] = jnp.broadcast_to(squares.scale(2 * ROWS, team * 2 * ROWS), m.scale.shape)
@@ -734,12 +747,12 @@
     stages = (
         (first, 0),
         (lambda c: hs.near(c, product), 2),
-        (lambda c: hs.own(c, product), 4),
-        (activate, 5),
-        (ring, 6),
-        (hg.hand_on, 7),
-        (down_near, 8),
-        (down_far, 9),
+        (lambda c: hs.own(c, product), 3),
+        (activate, 4),
+        (ring, 5),
+        (hg.hand_on, 6),
+        (down_near, 7),
+        (down_far, 8),
     )
 
     def turn(i, carry):
@@ -771,6 +784,23 @@
         piece.step_one()
     for piece in owns:
         piece.step_one()
+
+    def drain_chunk(c, carry):
+        hs.drain(c)
+        hg.drain(c)
+        for g in range(2):
+            given(c, g).wait_send()
+        lent(c).wait_send()
+        return carry
+
+    drain()
+    for copy in swaps + trades:
+        copy.wait_send()
+    for piece in near + away + scatter_a:
+        for copy in piece.copies():
+            copy.wait_send()
+    squares.drain()
+    lax.fori_loop(0, chunks, drain_chunk, 0)
     for piece in others:
         piece.step_two()
     for piece in owns:
@@ -784,25 +814,11 @@
         backs[h].wait_recv()
         m.out[h] = (value + m.back_in[h].astype(F32)).astype(BF)
 
-    def each(body):
-        lax.fori_loop(0, chunks, lambda c, carry: (body(c), carry)[1], 0)
-
-    drain()
-    for copy in swaps + trades + backs:
+    for copy in backs:
         copy.wait_send()
-    for piece in near + away + scatter_a + others + owns:
+    for piece in others + owns:
         for copy in piece.copies():
             copy.wait_send()
-    squares.drain()
-    each(hs.drain)
-    each(hg.drain)
-
-    def drain_given(c):
-        for g in range(2):
-            given(c, g).wait_send()
-        lent(c).wait_send()
-
-    each(drain_given)
 
 
 def reduce_scratch(name, chunks, columns, slots, rows):

time: 165 us -> 163 us (0.988)
  Pallas kernels: 163 us -> 161 us
    pallas_call x1, Pallas kernels: 163 us -> 161 us  [local_layer(): pl.pallas_call(functools.partial(kernel, (*inputs, 'out', *buffers)), nam...]
where the time goes in v5:
time: 163 us
  Pallas kernels  161 us (99%)
    pallas_call x1, Pallas kernels, local_layer(): pl.pallas_call(functools.partial(kernel, (*inputs, 'out', *buffers)), nam...  161 us

profile of v5, /device:TPU:1, one launch (start us, length us, event | category | flops | bytes accessed | tf_op | source)
XLA Modules:
  0.0 162.8 jit_solution(6683565262036686623)
XLA Ops:
  0.0 161.2 %layer.1 = bf16[2,64,512]{2,1,0:T(8,128)(2,1)} custom-call(bf16[2,64,512]{2,1,0:T(8,128)(2,1)} %bitcast.13, bf16[1,512]{1,0:T(2,128)(2,1)} %refs_1_.1, bf16[512,512]{1,0:T(8,128)(2,1)} %bitcast.11, bf16[2,512,512]{2,1,0:T(8,128)(2,1)} %bitcast.9, bf16[512,512]{1,0:T(8,128)(2,1)} %bitcast.12, bf16[1,512]{1,0:T(2,128)(2,1)} %refs_5_.1, ...), custom_call_target="tpu_custom_call" | custom-call | tf_op jit(solution)/shard_map/layer/pallas_call | solution.py:933
  161.2 1.6 copy.11

commit v6 on v5

--- a/solution.py
+++ b/solution.py
@@ -135,6 +135,7 @@
         self.at, self.part, self.pair, self.h = at, part, pair, h
         self.total, self.first, self.second = total, first, second
         self.mine, other = 2 * at.core + h, 2 * (1 - at.core) + h
+        self.other = other
         self.right, self.left, self.far = at.xi(1), at.xi(3), at.xi(2)
         self.half = ROWS // 2
 
@@ -161,9 +162,13 @@
         self.shares[i].wait_recv()
         return self.part[self.mine, self.rows(xx)].astype(F32) + self.pair[self.h, self.rows(xx)].astype(F32)
 
-    def start(self):
-        for copy in self.shares:
-            copy.start()
+    def start(self, late):
+        is_far = self.other == self.at.yi(2)
+
+        @pl.when(is_far if late else jnp.logical_not(is_far))
+        def _():
+            for copy in self.shares:
+                copy.start()
 
     def step_one(self):
         self.total[self.h, self.rows(self.far)] = self.summed(0, self.far).astype(BF)
@@ -371,7 +376,7 @@
     out[yy] = (wide * gain).astype(BF)
 
 
-def attention(at, m, spread, gain, spread_weights):
+def attention(at, m, spread, scatter, gain, spread_weights):
     half = HEAD // 2
     lane = lax.broadcasted_iota(jnp.int32, (1, HEAD), 1)
     base = [m.table[i, pl.ds(ROWS + at.dp, 1), :] for i in range(2)]
@@ -527,10 +532,14 @@
     project(at.y)
     project(at.yi(1))
     project(at.yi(3))
+    for piece in scatter:
+        piece.start(False)
     for k in range(RING):
         for copy in passes_of(k):
             copy.wait_recv()
     project(at.yi(2))
+    for piece in scatter:
+        piece.start(True)
 
     def drain():
         for copy in pending + list(lines_m.values()):
@@ -632,20 +641,16 @@
         swap.wait_recv()
         piece.start()
     spread_weights(0)
-    drain = attention(at, m, spread, m.gain_attn[...].astype(F32), spread_weights)
-
-    def scatters(part, pair, total, first, second, sems):
-        pieces = [Scatter(at, part, pair, total, first, second, h, sems) for h in range(2)]
-        for piece in pieces:
-            piece.start()
-        for piece in pieces:
-            piece.step_one()
-        for piece in pieces:
-            piece.step_two()
-        return pieces
+    scatter_a = [
+        Scatter(at, m.a_part, m.a_pair, m.a_total, m.a_first, m.a_second, h, m.ax) for h in range(2)
+    ]
+    drain = attention(at, m, spread, scatter_a, m.gain_attn[...].astype(F32), spread_weights)
 
     gain = m.gain_ffn[...].astype(F32)
-    scatter_a = scatters(m.a_part, m.a_pair, m.a_total, m.a_first, m.a_second, m.ax)
+    for piece in scatter_a:
+        piece.step_one()
+    for piece in scatter_a:
+        piece.step_two()
     trades = [
         send(m.f_gained.at[h], m.f_tokens.at[(1, *own[h])], m.trade, h, partner) for h in range(2)
     ]
@@ -743,7 +748,25 @@
     def row_scale():
         m.scale[...] = jnp.broadcast_to(squares.scale(2 * ROWS, team * 2 * ROWS), m.scale.shape)
 
-    once = ((squares.middle, 2), (row_scale, 4))
+    def both_sums():
+        sets = (
+            (m.g_part, m.g_pair, m.g_total, m.g_first, m.g_second, m.cx),
+            (m.f_part, m.f_pair, m.f_total, m.f_first, m.f_second, m.bx),
+        )
+        return [[Scatter(at, *refs[:5], h, refs[5]) for h in range(2)] for refs in sets]
+
+    def hand_over(blocks, late):
+        for j, part, pieces in zip((1, 0), (m.g_part, m.f_part), both_sums()):
+            for k in blocks:
+                part[at.yi(k)] = m.acc[j, k].astype(BF)
+            for piece in pieces:
+                piece.start(late)
+
+    once = (
+        (squares.middle, 2),
+        (row_scale, 4),
+        (lambda: hand_over((0, 1, 3), False), chunks + 7),
+    )
     stages = (
         (first, 0),
         (lambda c: hs.near(c, product), 2),
@@ -768,18 +791,8 @@
         return carry
 
     lax.fori_loop(0, chunks + stages[-1][1], turn, 0)
-    others = [
-        Scatter(at, m.g_part, m.g_pair, m.g_total, m.g_first, m.g_second, h, m.cx) for h in range(2)
-    ]
-    owns = [
-        Scatter(at, m.f_part, m.f_pair, m.f_total, m.f_first, m.f_second, h, m.bx) for h in range(2)
-    ]
-    for j, part, pieces in ((1, m.g_part, others), (0, m.f_part, owns)):
-        for yy, piece in zip((2 * (1 - at.core), 2 * (1 - at.core) + 1), pieces):
-            part[yy] = m.acc[j, lax.rem(yy - at.y + RING, RING)].astype(BF)
-            piece.start()
-        for yy in (2 * at.core, 2 * at.core + 1):
-            part[yy] = m.acc[j, lax.rem(yy - at.y + RING, RING)].astype(BF)
+    others, owns = both_sums()
+    hand_over((2,), True)
     for piece in others:
         piece.step_one()
     for piece in owns:

time: 163 us -> 162 us (level)
  no operation moved by 1% of the time
where the time goes in v6:
time: 162 us
  Pallas kernels  160 us (99%)
    pallas_call x1, Pallas kernels, local_layer(): pl.pallas_call(functools.partial(kernel, (*inputs, 'out', *buffers)), nam...  160 us

profile of v6, /device:TPU:1, one launch (start us, length us, event | category | flops | bytes accessed | tf_op | source)
XLA Modules:
  0.0 161.5 jit_solution(15676615555596923335)
XLA Ops:
  0.0 160.0 %layer.1 = bf16[2,64,512]{2,1,0:T(8,128)(2,1)} custom-call(bf16[2,64,512]{2,1,0:T(8,128)(2,1)} %bitcast.13, bf16[1,512]{1,0:T(2,128)(2,1)} %refs_1_.1, bf16[512,512]{1,0:T(8,128)(2,1)} %bitcast.11, bf16[2,512,512]{2,1,0:T(8,128)(2,1)} %bitcast.9, bf16[512,512]{1,0:T(8,128)(2,1)} %bitcast.12, bf16[1,512]{1,0:T(2,128)(2,1)} %refs_5_.1, ...), custom_call_target="tpu_custom_call" | custom-call | tf_op jit(solution)/shard_map/layer/pallas_call | solution.py:946
  160.0 1.6 copy.11

commit v7 on v6

--- a/solution.py
+++ b/solution.py
@@ -471,24 +471,24 @@
         queries = qs.result(c, own_rows) * scale
         pieces += [rotated(queries[:, h * HEAD : (h + 1) * HEAD], cosine, sine) for h in range(per)]
     stacked = jnp.concatenate(pieces, axis=0).astype(BF)
-    for copy in shares:
-        copy.wait_recv()
     row = lax.broadcasted_iota(jnp.int32, (RING * ROWS, GROUP), 0)
     col = lax.broadcasted_iota(jnp.int32, (RING * ROWS, GROUP), 1)
     query_at = lax.rem(row, ROWS) + at.dp * ROWS
     key_at = lax.div(col, ROWS) * GROUP + lax.rem(col, ROWS)
     weight = jnp.zeros((RING * ROWS, 1), F32)
-    for yy in range(RING):
+    arrivals = [at.yi(k) for k in (0, 2, 3, 1)]
+    for i, yy in enumerate(arrivals):
+        shares[i].wait_recv()
         raw = lax.dot_general(
             stacked, m.keys[0, yy], (((1,), (1,)), ((), ())), preferred_element_type=F32
         ) * HEAD ** (-0.5)
         kept = jnp.where(key_at + yy * ROWS <= query_at, jnp.exp(raw), 0.0)
-        m.scores[yy] = kept
+        m.scores[i] = kept
         weight = weight + jnp.sum(kept, axis=1, keepdims=True)
     mix = jnp.zeros((RING * ROWS, HEAD), F32)
-    for yy in range(RING):
+    for i, yy in enumerate(arrivals):
         mix = mix + jnp.dot(
-            (m.scores[yy] / weight).astype(BF), m.keys[1, yy], preferred_element_type=F32
+            (m.scores[i] / weight).astype(BF), m.keys[1, yy], preferred_element_type=F32
         )
 
     def rows_of(yy, k, start=0, count=ROWS):

time: 162 us -> 162 us (level)
  no operation moved by 1% of the time
where the time goes in v7:
time: 162 us
  Pallas kernels  160 us (99%)
    pallas_call x1, Pallas kernels, local_layer(): pl.pallas_call(functools.partial(kernel, (*inputs, 'out', *buffers)), nam...  160 us

profile of v7, /device:TPU:1, one launch (start us, length us, event | category | flops | bytes accessed | tf_op | source)
XLA Modules:
  0.0 161.9 jit_solution(4890544762237859597)
XLA Ops:
  0.0 160.3 %layer.1 = bf16[2,64,512]{2,1,0:T(8,128)(2,1)} custom-call(bf16[2,64,512]{2,1,0:T(8,128)(2,1)} %bitcast.13, bf16[1,512]{1,0:T(2,128)(2,1)} %refs_1_.1, bf16[512,512]{1,0:T(8,128)(2,1)} %bitcast.11, bf16[2,512,512]{2,1,0:T(8,128)(2,1)} %bitcast.9, bf16[512,512]{1,0:T(8,128)(2,1)} %bitcast.12, bf16[1,512]{1,0:T(2,128)(2,1)} %refs_5_.1, ...), custom_call_target="tpu_custom_call" | custom-call | tf_op jit(solution)/shard_map/layer/pallas_call | solution.py:946
  160.3 1.6 copy.11
